TPU v7x, 32 devices: a whole 2x2x4 slice. The times are simulated.
32 devices in a mesh: gx: 4 (over z), gy: 4 (over y, core), gz: 2 (over x).
Axes of the slice: x: 2, y: 2, z: 4, core: 2. Of those that a mesh axis runs over, the one named last changes fastest.
Arguments:
- velocities: float32 [3, 1310720], P(None, ('gx', 'gy', 'gz')), may hold values from -6 to 6
- particle_cells: int32 [2, 1310720], P(None, ('gx', 'gy', 'gz')), may hold values from 0 to 4095
- grid_shift: int32 [2, 3], replicated, may hold values from -1 to 1, as said below
- axis_index: int32 [2, 16, 32, 256], P(None, 'gx', 'gy', 'gz'), may hold values from 0 to 7
- migrate_dir: int32 [1310720], P(('gx', 'gy', 'gz')), may hold values from 0 to 6, as said below
- migrate_slot: int32 [1310720], P(('gx', 'gy', 'gz')), may hold values from 0 to 159, as said below
- contact_colloid: int32 [65536], P(('gx', 'gy', 'gz')), may hold values from 0 to 8191, as said below
- contact_particle: int32 [65536], P(('gx', 'gy', 'gz')), may hold values from 0 to 40959
- contact_weight: float32 [65536], P(('gx', 'gy', 'gz')), may hold values from 0.05 to 1
- colloid_velocity: float32 [3, 8192], P(None, ('gx', 'gy', 'gz')), may hold values from -6 to 6
Outputs:
- cell_velocity: float32 [3, 16, 32, 256], P(None, 'gx', 'gy', 'gz')
- migrated: float32 [3, 1341440], P(None, ('gx', 'gy', 'gz'))
- colloid_force: float32 [3, 8192], P(None, ('gx', 'gy', 'gz'))
Inputs may be any that keep to these rules, and one draw needn't show every extreme that they name: `grid_shift`: every entry is -1 or 1, and along every dimension the sign changes from each step to the next. `migrate_dir`: code 0 keeps a particle on its device. On every device at most 160 particles take any one nonzero code, and on every device some nonzero code is taken by exactly 160 particles. `migrate_slot`: among the particles of one device with the same nonzero code, the slots are distinct and run from 0 to that code's count minus 1; the slot is 0 where the code is 0. `contact_colloid`: the owner of every contact's colloid is the contact's own device or one of its six face neighbours along gx, gy, gz (periodic).
All inputs are finite; a program needn't handle non-finite values.
Results may differ from a plain program's by a relative error of at most 0.00015.
Values sent between devices are 32-bit elements; how exact they have to be, the bound alone decides.
A program may use at most 128 MiB of HBM per device.

v0:
```python
import math

import jax
import jax.numpy as jnp
import numpy as np
from jax import lax
from jax.sharding import PartitionSpec as P

COLLOIDS_PER_UNIT = 256
CAP = 160


SEND_PLACES = ((1, 0, 0), (0, 1, 1), (0, 1, 0), (1, 0, 1), (0, 0, 1), (1, 1, 0))
TAKE_PLACES = ((0, 1, 1), (3, 2, 2), (1, 0, 1), (2, 3, 2), (1, 1, 0), (2, 2, 3))


def with_halo(block, sides, width):
    for axis, dim in sides:
        count = lax.axis_size(axis)
        forward = [(i, i + 1) for i in range(count - 1)]
        forward.append((count - 1, 0))
        backward = [(target, source) for source, target in forward]
        low = lax.ppermute(
            lax.slice_in_dim(block, block.shape[dim] - width, None, axis=dim), axis, forward
        )
        high = lax.ppermute(lax.slice_in_dim(block, 0, width, axis=dim), axis, backward)
        block = jnp.concatenate([low, block, high], axis=dim)
    return block


def rotation_table():
    angle = 130.0 * math.pi / 180.0
    cosine = math.cos(angle)
    sine_value = math.sin(angle)
    entries = []
    for number in range(8):
        signs = [1.0 if number >> bit & 1 else -1.0 for bit in range(3)]
        unit = np.array(signs) / math.sqrt(3.0)
        cross = np.array(
            [[0.0, -unit[2], unit[1]], [unit[2], 0.0, -unit[0]], [-unit[1], unit[0], 0.0]]
        )
        matrix = cosine * np.eye(3) + (1.0 - cosine) * np.outer(unit, unit) + sine_value * cross
        entries.append(matrix.reshape(9))
    return np.array(entries)


def cell_rotation(axis_ids, table):
    matrix = jnp.zeros((9,) + axis_ids.shape, jnp.float32)
    for number in range(8):
        chosen = jnp.where(axis_ids == number, 1.0, 0.0).astype(jnp.float32)
        matrix = matrix + chosen[None] * table[number].reshape((9,) + (1,) * axis_ids.ndim)
    return matrix


def apply_rotation(matrix, vector):
    rows = [
        matrix[3 * row] * vector[0]
        + matrix[3 * row + 1] * vector[1]
        + matrix[3 * row + 2] * vector[2]
        for row in range(3)
    ]
    return jnp.stack(rows)


def fold_rims(field, axis, length):
    lower = lax.slice_in_dim(field, 0, 1, axis=axis)
    inner = lax.slice_in_dim(field, 2, length + 2, axis=axis)
    upper = lax.slice_in_dim(field, length + 3, length + 4, axis=axis)
    low_widths = [(0, 0)] * field.ndim
    low_widths[axis] = (0, length - 1)
    high_widths = [(0, 0)] * field.ndim
    high_widths[axis] = (length - 1, 0)
    return inner + jnp.pad(lower, low_widths) + jnp.pad(upper, high_widths)


def face_cube(blocks):
    cube = jnp.zeros((2, 2, 2) + blocks[0].shape, jnp.float32)
    for place, block in zip(SEND_PLACES, blocks):
        cube = cube.at[place].set(block)
    return cube


def face_take(beside_all):
    return [beside_all[place] for place in TAKE_PLACES]


def body(
    velocities,
    particle_cells,
    grid_shift,
    axis_index,
    migrate_dir,
    migrate_slot,
    contact_colloid,
    contact_particle,
    contact_weight,
    colloid_velocity,
):
    table = jnp.asarray(rotation_table(), jnp.float32)
    cells_x, cells_y, cells_z = (axis_index.shape[1], axis_index.shape[2], axis_index.shape[3])
    extent = (cells_x + 2, cells_y + 2, cells_z + 2)
    extent_total = extent[0] * extent[1] * extent[2]
    velocity_now = velocities
    mean = jnp.zeros((3, cells_x, cells_y, cells_z), jnp.float32)
    for step in range(particle_cells.shape[0]):
        local = particle_cells[step]
        place_x = local // (cells_y * cells_z) + grid_shift[step, 0] + 1
        place_y = local // cells_z % cells_y + grid_shift[step, 1] + 1
        place_z = local % cells_z + grid_shift[step, 2] + 1
        wide_cell = (place_x * extent[1] + place_y) * extent[2] + place_z
        momentum = (
            jnp.zeros((3, extent_total), jnp.float32)
            .at[:, wide_cell]
            .add(velocity_now)
            .reshape((3,) + extent)
        )
        counts = (
            jnp.zeros((1, extent_total), jnp.float32)
            .at[:, wide_cell]
            .add(1.0)
            .reshape((1,) + extent)
        )
        momentum, counts = (
            with_halo(momentum, (("gx", 1), ("gy", 2), ("gz", 3)), 1),
            with_halo(counts, (("gx", 1), ("gy", 2), ("gz", 3)), 1),
        )
        for axis, length in ((1, cells_x), (2, cells_y), (3, cells_z)):
            momentum = fold_rims(momentum, axis, length)
            counts = fold_rims(counts, axis, length)
        mean = momentum / jnp.maximum(counts, 1.0)
        matrix = cell_rotation(axis_index[step], table)
        offset = mean - apply_rotation(matrix, mean)
        packed = jnp.concatenate([matrix, offset], axis=0)
        beside_all = with_halo(packed, (("gx", 1), ("gy", 2), ("gz", 3)), 1)
        reach = beside_all.reshape(12, extent_total)
        picked = reach[:, wide_cell]
        velocity_now = apply_rotation(picked[:9], velocity_now) + picked[9:]
    size_x = lax.axis_size("gx")
    size_y = lax.axis_size("gy")
    size_z = lax.axis_size("gz")
    mine_x = lax.axis_index("gx")
    mine_y = lax.axis_index("gy")
    mine_z = lax.axis_index("gz")
    leaving = migrate_dir > 0
    target = jnp.where(leaving, (migrate_dir - 1) * CAP + migrate_slot, 6 * CAP)
    blocks = (
        jnp.zeros((3, 6 * CAP), jnp.float32)
        .at[:, target]
        .set(velocity_now, mode="drop")
        .reshape(3, 6, CAP)
    )
    kept = jnp.where(leaving[None], 0.0, velocity_now)
    cube = face_cube([blocks[:, number] for number in range(6)])
    beside_all = with_halo(cube, (("gx", 0), ("gy", 1), ("gz", 2)), 1)
    arrivals = jnp.stack(face_take(beside_all), axis=1)
    migrated = jnp.concatenate([kept, arrivals.reshape(3, 6 * CAP)], axis=1)
    weighted = contact_weight[None] * velocity_now[:, contact_particle]
    owning_device = contact_colloid // COLLOIDS_PER_UNIT
    apart_x = (owning_device // (size_y * size_z) - mine_x) % size_x
    apart_y = (owning_device // size_z % size_y - mine_y) % size_y
    apart_z = (owning_device % size_z - mine_z) % size_z
    slot_code = jnp.where(
        apart_x == 1,
        1,
        jnp.where(
            apart_x == size_x - 1,
            2,
            jnp.where(
                apart_y == 1,
                3,
                jnp.where(
                    apart_y == size_y - 1,
                    4,
                    jnp.where(apart_z == 1, 5, jnp.where(apart_z == size_z - 1, 6, 0)),
                ),
            ),
        ),
    )
    position = slot_code * COLLOIDS_PER_UNIT + contact_colloid % COLLOIDS_PER_UNIT
    sums = (
        jnp.zeros((3, 7 * COLLOIDS_PER_UNIT), jnp.float32)
        .at[:, position]
        .add(weighted)
        .reshape(3, 7, COLLOIDS_PER_UNIT)
    )
    weight_sums = (
        jnp.zeros((1, 7 * COLLOIDS_PER_UNIT), jnp.float32)
        .at[:, position]
        .add(contact_weight[None])
        .reshape(1, 7, COLLOIDS_PER_UNIT)
    )
    cube_sums = face_cube([sums[:, number + 1] for number in range(6)])
    cube_weights = face_cube([weight_sums[:, number + 1] for number in range(6)])
    around_sums, around_weights = (
        with_halo(cube_sums, (("gx", 0), ("gy", 1), ("gz", 2)), 1),
        with_halo(cube_weights, (("gx", 0), ("gy", 1), ("gz", 2)), 1),
    )
    sum_wv = sums[:, 0]
    sum_w = weight_sums[:, 0]
    for piece in face_take(around_sums):
        sum_wv = sum_wv + piece
    for piece in face_take(around_weights):
        sum_w = sum_w + piece
    colloid_force = (sum_wv - sum_w * colloid_velocity) / jnp.maximum(sum_w, 1.0)
    return (mean, migrated, colloid_force)


def solution(mesh):
    placed = (
        P(None, ("gx", "gy", "gz")),
        P(None, ("gx", "gy", "gz")),
        P(),
        P(None, "gx", "gy", "gz"),
        P(("gx", "gy", "gz")),
        P(("gx", "gy", "gz")),
        P(("gx", "gy", "gz")),
        P(("gx", "gy", "gz")),
        P(("gx", "gy", "gz")),
        P(None, ("gx", "gy", "gz")),
    )
    return jax.shard_map(
        body,
        mesh=mesh,
        in_specs=placed,
        out_specs=(
            P(None, "gx", "gy", "gz"),
            P(None, ("gx", "gy", "gz")),
            P(None, ("gx", "gy", "gz")),
        ),
        check_vma=False,
    )
```

profile of v0, /device:TPU:0, one launch (start us, length us, event | category | flops | bytes accessed | tf_op | source)
XLA Modules:
  0.0 1522.1 jit_solution(16184611651690890855)
XLA Ops:
  0.6 1.6 fusion.147
  2.2 10.3 compare_select_fusion
  12.5 213.7 %scatter_custom_fusion.1 = f32[7800]{0:T(1024)S(1)} fusion(s32[40960]{0:T(1024)S(1)} %bitcast.198, f32[40960]{0:T(1024)S(1)} %broadcast.921, f32[]{:T(128)} %constant.647.clone.1), kind=kCustom, calls=%fused_computation.246 | custom fusion | flops 40960 | bytes 31204 | tf_op jit(solution)/shard_map/scatter-add | solution.py:120
  226.4 3.1 collective-permute-start.6
  229.5 2.1 collective-permute-start.7
  231.6 213.7 %scatter_custom_fusion.3 = f32[7800]{0:T(1024)S(1)} fusion(s32[40960]{0:T(1024)S(1)} %bitcast.195, f32[40960]{0:T(1024)S(1)} %broadcast.921, f32[]{:T(128)} %constant.647.clone.1), kind=kCustom, calls=%fused_computation.244 | custom fusion | flops 40960 | bytes 31204 | tf_op jit(solution)/shard_map/scatter-add | solution.py:120
  445.5 3.8 collective-permute-start.25
  449.4 11.1 copy.129
  460.4 219.8 %scatter_custom_fusion = f32[3,7800]{0,1:T(8,128)} fusion(s32[40960]{0:T(1024)S(1)} %bitcast.199, f32[40960,3]{1,0:T(8,128)} %copy.129, f32[]{:T(128)} %constant.647.clone.1), kind=kCustom, calls=%fused_computation.12 | custom fusion | flops 122880 | bytes 94112 | tf_op jit(solution)/shard_map/scatter-add | solution.py:114
  680.3 3.1 copy.130
  684.0 11.3 scatter_custom_fusion.6
  697.0 3.9 collective-permute-start.1
  701.1 1.8 collective-permute-start.9
  704.3 1.7 collective-permute-start.27
  707.2 1.6 collective-permute-start.10
  709.4 2.1 collective-permute-done.10
  711.5 1.6 collective-permute-start.28
  714.4 1.5 collective-permute-done.28
  715.9 4.1 collective-permute-start.49
  720.6 1.7 collective-permute-start.3
  724.0 1.6 collective-permute-start.4
  726.2 4.7 collective-permute-done.4
  730.9 4.2 collective-permute-done.5
  736.1 3.8 collective-permute-start.13
  740.6 1.9 collective-permute-done.12
  742.6 1.7 collective-permute-start.15
  744.5 1.5 collective-permute-done.14
  754.7 3.0 copy.135
  757.7 137.2 %gather_fusion = f32[40960,12]{1,0:T(8,128)} fusion(f32[12,7800]{0,1:T(8,128)} %copy.135, s32[40960]{0:T(1024)S(1)} %broadcast_clamp_fusion.1), kind=kCustom, calls=%fused_computation | custom fusion | bytes 4096000 | tf_op jit(solution)/shard_map/gather | solution.py:136
  894.9 11.5 copy.136
  909.1 10.0 copy.137
  919.1 219.7 %scatter_custom_fusion.2 = f32[3,7800]{0,1:T(8,128)} fusion(s32[40960]{0:T(1024)} %bitcast.197, f32[40960,3]{1,0:T(8,128)} %copy.137, f32[]{:T(128)} %constant.647.clone.1), kind=kCustom, calls=%fused_computation.10 | custom fusion | flops 122880 | bytes 94112 | tf_op jit(solution)/shard_map/scatter-add | solution.py:114
  1138.8 2.9 copy.138
  1142.1 9.7 collective-permute-start.18
  1153.6 3.7 collective-permute-start.19
  1159.2 1.7 collective-permute-start.21
  1161.0 1.5 collective-permute-done.20
  1166.9 2.5 collective-permute-done.22
  1169.4 4.2 collective-permute-done.23
  1174.5 1.9 collective-permute-start.30
  1176.3 2.4 collective-permute-start.31
  1179.4 1.4 collective-permute-done.30
  1182.0 1.7 collective-permute-start.33
  1183.7 1.6 collective-permute-done.32
  1187.7 2.1 copy.139
  1191.5 1.5 collective-permute-start.35
  1193.0 1.6 slice_add_fusion.1
  1194.6 1.6 copy.141
  1196.1 1.6 copy.142
  1197.7 1.7 pad_maximum_fusion.1
  1199.8 3.0 copy.143
  1202.8 137.2 %gather_fusion.1 = f32[40960,12]{1,0:T(8,128)} fusion(f32[12,7800]{0,1:T(8,128)} %copy.143, s32[40960]{0:T(1024)S(1)} %copy-done.5), kind=kCustom, calls=%fused_computation.1 | custom fusion | bytes 4096000 | tf_op jit(solution)/shard_map/gather | solution.py:136
  1340.0 11.4 copy.144
  1351.4 1.4 fusion.37
  1352.9 1.5 broadcast_select_fusion
  1354.4 10.0 copy.155
  1364.4 24.5 %scatter_custom_fusion.5 = f32[3,1792]{0,1:T(8,128)S(1)} fusion(s32[2048]{0:T(1024)} %copy-done.20, f32[2048]{0:T(1024)S(1)} %copy-done.17, f32[]{:T(128)} %constant.647.clone.1, f32[3,40960]{0,1:T(8,128)} %copy.155, s32[2048]{0:T(1024)S(1)} %get-tuple-element.341), kind=kCustom, calls=%fused_computation.16 | custom fusion | flops 12288 | bytes 21009920 | tf_op jit(solution)/shard_map/scatter-add | solution.py:183
  1389.5 10.0 copy.145
  1399.6 100.4 %scatter_custom_fusion.4 = f32[3,960]{0,1:T(8,128)S(1)} fusion(s32[40960]{0:T(1024)} %compare_select_fusion.6, f32[40960,3]{1,0:T(8,128)} %copy.145, f32[]{:T(128)} %constant.647.clone.1), kind=kCustom, calls=%fused_computation.45 | custom fusion | bytes 12032 | tf_op jit(solution)/shard_map/scatter | solution.py:149
  1502.1 2.6 collective-permute-start.37
  1504.8 3.8 collective-permute-start.43
  1508.9 1.8 collective-permute-start.39
  1517.0 1.6 collective-permute-done.40
  1519.7 1.6 collective-permute-done.47
  (294 shorter events, 49.3 us)
Async XLA Ops:
  12.5 727.4 %copy-start.6 = (s32[40960,1]{0,1:T(1,128)}, s32[40960,1]{0,1:T(1,128)S(1)}, u32[]{:S(2)}) copy-start(s32[40960,1]{0,1:T(1,128)S(1)} %get-tuple-element.261) | copy-start | bytes 491524
  226.4 470.5 %collective-permute-start.6 = (f32[1,1,10,130]{3,2,1,0:T(8,128)S(1)}, f32[1,1,10,130]{3,2,1,0:T(8,128)S(1)}, u32[]{:S(2)}, u32[]{:S(2)}) collective-permute-start(f32[1,1,10,130]{3,2,1,0:T(8,128)S(1)} %get-tuple-element.295), channel_id=1, source_target_pairs={{0,8},{8,16},{16,24},{24,0},{1,9},{9,17},{17,25},{25,1},{2,10},{10... | collective-permute-start | bytes 15608 | tf_op jit(solution)/shard_map/ppermute | solution.py:23
  229.5 471.4 %collective-permute-start.7 = (f32[1,1,10,130]{3,2,1,0:T(8,128)S(1)}, f32[1,1,10,130]{3,2,1,0:T(8,128)S(1)}, u32[]{:S(2)}, u32[]{:S(2)}) collective-permute-start(f32[1,1,10,130]{3,2,1,0:T(8,128)S(1)} %get-tuple-element.294), channel_id=1, source_target_pairs={{8,0},{16,8},{24,16},{0,24},{9,1},{17,9},{25,17},{1,25},{10,2},{18... | collective-permute-start | bytes 15608 | tf_op jit(solution)/shard_map/ppermute | solution.py:26
  445.5 255.6 %collective-permute-start.24 = (f32[1,1,10,130]{3,2,1,0:T(8,128)S(1)}, f32[1,1,10,130]{3,2,1,0:T(8,128)S(1)}, u32[]{:S(2)}, u32[]{:S(2)}) collective-permute-start(f32[1,1,10,130]{3,2,1,0:T(8,128)S(1)} %get-tuple-element.293), channel_id=1, source_target_pairs={{0,8},{8,16},{16,24},{24,0},{1,9},{9,17},{17,25},{25,1},{2,10},{10... | collective-permute-start | bytes 15608 | tf_op jit(solution)/shard_map/ppermute | solution.py:23
  445.5 255.6 %collective-permute-start.25 = (f32[1,1,10,130]{3,2,1,0:T(8,128)S(1)}, f32[1,1,10,130]{3,2,1,0:T(8,128)S(1)}, u32[]{:S(2)}, u32[]{:S(2)}) collective-permute-start(f32[1,1,10,130]{3,2,1,0:T(8,128)S(1)} %get-tuple-element.292), channel_id=1, source_target_pairs={{8,0},{16,8},{24,16},{0,24},{9,1},{17,9},{25,17},{1,25},{10,2},{18... | collective-permute-start | bytes 15608 | tf_op jit(solution)/shard_map/ppermute | solution.py:26
  680.2 16.5 %copy-start.26 = (f32[9]{0:T(128)S(1)}, f32[9]{0:T(128)}, u32[]{:S(2)}) copy-start(f32[9]{0:T(128)} %constant.708) | copy-start | bytes 112
  680.2 16.5 %copy-start.27 = (f32[9]{0:T(128)S(1)}, f32[9]{0:T(128)}, u32[]{:S(2)}) copy-start(f32[9]{0:T(128)} %constant.710) | copy-start | bytes 112
  680.2 16.5 %copy-start.28 = (f32[9]{0:T(128)S(1)}, f32[9]{0:T(128)}, u32[]{:S(2)}) copy-start(f32[9]{0:T(128)} %constant.712) | copy-start | bytes 112
  683.4 36.8 %copy-start.21 = (pred[4]{0:T(512)(128)(4,1)S(1)}, pred[4]{0:T(512)(128)(4,1)}, u32[]{:S(2)}) copy-start(pred[4]{0:T(512)(128)(4,1)} %constant.665.clone.1) | copy-start | bytes 16
  683.7 36.6 %collective-permute-start = (f32[3,1,10,130]{3,2,1,0:T(8,128)S(1)}, f32[3,1,10,130]{3,2,1,0:T(8,128)S(1)}, u32[]{:S(2)}, u32[]{:S(2)}) collective-permute-start(f32[3,1,10,130]{3,2,1,0:T(8,128)S(1)} %get-tuple-element.269), channel_id=1, source_target_pairs={{0,8},{8,16},{16,24},{24,0},{1,9},{9,17},{17,25},{25,1},{2,10},{10... | collective-permute-start | bytes 46808 | tf_op jit(solution)/shard_map/ppermute | solution.py:23
  684.0 38.3 %copy-start.22 = (pred[8]{0:T(512)(128)(4,1)S(1)}, pred[8]{0:T(512)(128)(4,1)}, u32[]{:S(2)}) copy-start(pred[8]{0:T(512)(128)(4,1)} %constant.666.clone.1) | copy-start | bytes 28
  697.0 23.5 %collective-permute-start.1 = (f32[3,1,10,130]{3,2,1,0:T(8,128)S(1)}, f32[3,1,10,130]{3,2,1,0:T(8,128)S(1)}, u32[]{:S(2)}, u32[]{:S(2)}) collective-permute-start(f32[3,1,10,130]{3,2,1,0:T(8,128)S(1)} %get-tuple-element.268), channel_id=1, source_target_pairs={{8,0},{16,8},{24,16},{0,24},{9,1},{17,9},{25,17},{1,25},{10,2},{18... | collective-permute-start | bytes 46808 | tf_op jit(solution)/shard_map/ppermute | solution.py:26
  700.9 48.5 %collective-permute-start.48 = (f32[1,2,2,1,256]{4,3,2,1,0:T(1,128)S(1)}, f32[1,2,2,1,256]{4,3,2,1,0:T(1,128)S(1)}, u32[]{:S(2)}, u32[]{:S(2)}) collective-permute-start(f32[1,2,2,1,256]{4,3,2,1,0:T(1,128)S(1)} %get-tuple-element.326), channel_id=1, source_target_pairs={{0,8},{8,16},{16,24},{24,0},{1,9},{9,17},{17,25},{25,1},{2,10},{10... | collective-permute-start | bytes 12296 | tf_op jit(solution)/shard_map/ppermute | solution.py:23
  701.0 3.1 collective-permute-start.8
  701.1 3.1 collective-permute-start.9
  704.2 3.1 collective-permute-start.26
  704.3 4.6 collective-permute-start.27
  706.1 20.0 %copy-start.16 = (pred[128]{0:T(512)(128)(4,1)S(1)}, pred[128]{0:T(512)(128)(4,1)}, u32[]{:S(2)}) copy-start(pred[128]{0:T(512)(128)(4,1)} %constant.667.clone.1) | copy-start | bytes 388
  707.2 4.3 collective-permute-start.10
  708.9 4.5 collective-permute-start.11
  711.5 4.4 collective-permute-start.28
  713.4 6.7 collective-permute-start.29
  715.9 33.4 %collective-permute-start.49 = (f32[1,2,2,1,256]{4,3,2,1,0:T(1,128)S(1)}, f32[1,2,2,1,256]{4,3,2,1,0:T(1,128)S(1)}, u32[]{:S(2)}, u32[]{:S(2)}) collective-permute-start(f32[1,2,2,1,256]{4,3,2,1,0:T(1,128)S(1)} %get-tuple-element.327), channel_id=1, source_target_pairs={{8,0},{16,8},{24,16},{0,24},{9,1},{17,9},{25,17},{1,25},{10,2},{18... | collective-permute-start | bytes 12296 | tf_op jit(solution)/shard_map/ppermute | solution.py:26
  720.5 3.3 collective-permute-start.2
  720.6 3.3 collective-permute-start.3
  724.0 6.9 collective-permute-start.4
  725.6 9.5 collective-permute-start.5
  736.0 6.5 collective-permute-start.12
  736.1 6.4 collective-permute-start.13
  742.6 3.4 collective-permute-start.14
  742.6 3.4 collective-permute-start.15
  746.8 3.9 collective-permute-start.16
  748.6 3.9 collective-permute-start.17
  1142.1 16.0 %collective-permute-start.18 = (f32[3,1,10,130]{3,2,1,0:T(8,128)S(1)}, f32[3,1,10,130]{3,2,1,0:T(8,128)S(1)}, u32[]{:S(2)}, u32[]{:S(2)}) collective-permute-start(f32[3,1,10,130]{3,2,1,0:T(8,128)S(1)} %get-tuple-element.265), channel_id=1, source_target_pairs={{0,8},{8,16},{16,24},{24,0},{1,9},{9,17},{17,25},{25,1},{2,10},{10... | collective-permute-start | bytes 46808 | tf_op jit(solution)/shard_map/ppermute | solution.py:23
  1151.8 9.1 collective-permute-start.50
  1152.3 8.6 collective-permute-start.51
  1153.6 5.5 collective-permute-start.19
  1159.1 3.3 collective-permute-start.20
  1159.2 3.3 collective-permute-start.21
  1162.5 21.2 %copy-start.25 = (f32[1,1,256]{2,1,0:T(1,128)S(1)}, f32[1,1,256]{2,1,0:T(1,128)}, u32[]{:S(2)}) copy-start(f32[1,1,256]{2,1,0:T(1,128)} %get-tuple-element.324) | copy-start | bytes 3076
  1162.7 6.7 collective-permute-start.22
  1163.5 10.1 collective-permute-start.23
  1164.8 14.6 collective-permute-start.52
  1165.6 13.8 collective-permute-start.53
  1174.5 6.4 collective-permute-start.30
  1176.3 5.5 collective-permute-start.31
  1181.9 3.4 collective-permute-start.32
  1182.0 3.4 collective-permute-start.33
  1189.9 4.7 collective-permute-start.34
  1191.5 4.7 collective-permute-start.35
  1399.6 119.1 %copy-start = (f32[3,40960]{1,0:T(4,128)S(1)}, f32[3,40960]{1,0:T(4,128)}, u32[]{:S(2)}) copy-start(f32[3,40960]{1,0:T(4,128)} %get-tuple-element.227) | copy-start | bytes 1474564
  1399.6 121.7 %copy-start.24 = (f32[3,256]{1,0:T(4,128)S(1)}, f32[3,256]{1,0:T(4,128)}, u32[]{:S(2)}) copy-start(f32[3,256]{1,0:T(4,128)} %param.56) | copy-start | bytes 9220
  1500.8 7.9 collective-permute-start.36
  1502.1 6.6 collective-permute-start.37
  1504.8 5.9 collective-permute-start.42
  1504.8 5.9 collective-permute-start.43
  1508.8 3.7 collective-permute-start.38
  1508.9 3.6 collective-permute-start.39
  1510.7 4.1 collective-permute-start.44
  1511.4 3.5 collective-permute-start.45
  1512.7 4.3 collective-permute-start.41
  1514.1 4.5 collective-permute-start.40
  1514.9 4.8 collective-permute-start.46
  1516.3 5.0 collective-permute-start.47
  (24 other events, 214.5 us)
where the time goes:
time: 1530 us; the launch traced here: 1520 us
  other arithmetic  929 us (61%)
  local copies, waits for them, and re-layouts  470 us (31%)
  starting transfers between devices  81.8 us (5%)
  waiting for transfers between devices  39.4 us (3%)
    scatter-add x2, other arithmetic, body(): momentum = jnp.zeros((3, extent_total), jnp.float32).at[:, wide_cell].add...  439 us
    scatter-add x2, other arithmetic, body(): counts = jnp.zeros((1, extent_total), jnp.float32).at[:, wide_cell].add(1...  427 us
    gather x4, local copies, waits for them, and re-layouts, body(): picked = reach[:, wide_cell]  297 us
    scatter x1, local copies, waits for them, and re-layouts, body(): blocks = jnp.zeros((3, 6 * CAP), jnp.float32).at[:, target].set(velocity_...  100 us
    ppermute x27, starting transfers between devices, with_halo(): lax.ppermute(lax.slice_in_dim(block, 0, width, axis=dim), axis, backward)  53.5 us
  transfers between devices with their start and end apart: 54, of which 23 were waited for; matrix products, arithmetic and copies ran while one was open for 31% of the time, Pallas kernels for 0%

commit v1 on v0

v1 whole, which is shorter than its diff:
```python
import functools
import math

import jax
import jax.numpy as jnp
from jax import lax
from jax.experimental import pallas as pl
from jax.experimental.pallas import tpu as pltpu
from jax.sharding import PartitionSpec as P

CAP = 160
ANGLE = 130.0 * math.pi / 180.0
COS, SIN = math.cos(ANGLE), math.sin(ANGLE)
TILE = 2048
NT = (((1,), (1,)), ((), ()))
BF = jnp.bfloat16
F32 = jnp.float32


def split_index(c, low):
    if low & (low - 1) == 0:
        return c >> (low.bit_length() - 1), c & (low - 1)
    return c // low, c % low


def one_hot(row, count):
    wide = lax.broadcasted_iota(jnp.int32, (count, row.shape[1]), 0)
    return jnp.where(wide == row, 1.0, 0.0).astype(BF)


def halves(x):
    high = x.astype(BF)
    return high, (x - high.astype(F32)).astype(BF)


def spread(rows, mask):
    return jnp.concatenate([mask * row for row in rows], axis=0)


def hist_tile(c, v, nhi, nlo):
    hi, lo = split_index(c, nlo)
    mask = one_hot(hi, nhi)
    rows = []
    for k in range(3):
        rows.extend(halves(v[k]))
    left = jnp.concatenate([spread(rows, mask), mask], axis=0)
    return lax.dot_general(left, one_hot(lo, nlo), NT, preferred_element_type=F32)


def mean_of(acc, mean_ref, nhi):
    count = jnp.maximum(acc[6 * nhi : 7 * nhi], 1.0)
    for k in range(3):
        total = acc[2 * k * nhi : (2 * k + 1) * nhi] + acc[(2 * k + 1) * nhi : (2 * k + 2) * nhi]
        mean_ref[k] = total / count


def signs_of(index):
    return [jnp.where((index & (1 << i)) != 0, 1.0, -1.0) for i in range(3)]


def rotate(e, v):
    along = ((1.0 - COS) / 3.0) * (e[0] * v[0] + e[1] * v[1] + e[2] * v[2])
    turn = SIN / math.sqrt(3.0)
    out = []
    for i in range(3):
        j, k = (i + 1) % 3, (i + 2) % 3
        out.append(COS * v[i] + e[i] * along + turn * (e[j] * v[k] - e[k] * v[j]))
    return out


def make_table(mean_ref, axis_ref, table_ref, nhi, nlo):
    mean = [mean_ref[k] for k in range(3)]
    index = axis_ref[...]
    turned = rotate(signs_of(index), mean)
    for k in range(3):
        high, low = halves(mean[k] - turned[k])
        table_ref[k * nhi : (k + 1) * nhi, 0:nlo] = high
        table_ref[k * nhi : (k + 1) * nhi, nlo : 2 * nlo] = low
    table_ref[3 * nhi : 4 * nhi, 0:nlo] = index.astype(F32).astype(BF)
    table_ref[3 * nhi : 4 * nhi, nlo : 2 * nlo] = jnp.zeros((nhi, nlo), BF)


def collide_tile(c, v, table, nhi, nlo):
    hi, lo = split_index(c, nlo)
    hot = one_hot(lo, nlo)
    got = jnp.dot(table, jnp.concatenate([hot, hot], axis=0), preferred_element_type=F32)
    here = lax.broadcasted_iota(jnp.int32, (nhi, c.shape[1]), 0) == hi
    picked = [
        jnp.sum(jnp.where(here, got[q * nhi : (q + 1) * nhi], 0.0), axis=0, keepdims=True)
        for q in range(4)
    ]
    turned = rotate(signs_of(picked[3].astype(jnp.int32)), v)
    return [turned[k] + picked[k] for k in range(3)]


def rows3(ref, at):
    return [ref[k : k + 1, at] for k in range(3)]


def first_kernel(tile, nhi, nlo, cell_ref, v_ref, mean_ref, acc):
    acc[...] = jnp.zeros_like(acc)

    def step(t, carry):
        at = pl.ds(pl.multiple_of(t * tile, tile), tile)
        acc[...] += hist_tile(cell_ref[0:1, at], rows3(v_ref, at), nhi, nlo)
        return carry

    lax.fori_loop(0, v_ref.shape[1] // tile, step, 0)
    mean_of(acc, mean_ref, nhi)


def middle_kernel(
    tile, nhi, nlo, cell_ref, v_ref, mean_ref, axis_ref, next_ref, next_mean_ref, acc, table_ref
):
    acc[...] = jnp.zeros_like(acc)
    make_table(mean_ref, axis_ref, table_ref, nhi, nlo)

    def step(t, carry):
        at = pl.ds(pl.multiple_of(t * tile, tile), tile)
        new = collide_tile(cell_ref[0:1, at], rows3(v_ref, at), table_ref[...], nhi, nlo)
        for k in range(3):
            next_ref[k : k + 1, at] = new[k]
        acc[...] += hist_tile(cell_ref[1:2, at], new, nhi, nlo)
        return carry

    lax.fori_loop(0, v_ref.shape[1] // tile, step, 0)
    mean_of(acc, next_mean_ref, nhi)


def last_kernel(
    tile, nhi, nlo, units, cell_ref, v_ref, mean_ref, axis_ref, dir_ref, slot_ref, place_ref, who_ref,
    weight_ref, kept_ref, o0, o1, o2, o3, o4, o5, own_ref, moved, table_ref, seen
):
    moved[...] = jnp.zeros_like(moved)
    make_table(mean_ref, axis_ref, table_ref, nhi, nlo)
    per = tile // 128

    def step(t, carry):
        at = pl.ds(pl.multiple_of(t * tile, tile), tile)
        new = collide_tile(cell_ref[1:2, at], rows3(v_ref, at), table_ref[...], nhi, nlo)
        code = dir_ref[0:1, at]
        stays = code == 0
        rows = []
        for k in range(3):
            kept_ref[k : k + 1, at] = jnp.where(stays, new[k], 0.0)
            rows.extend(halves(new[k]))
            for j in range(per):
                seen[k, pl.ds(t * per + j, 1), :] = new[k][:, j * 128 : (j + 1) * 128]
        mask = one_hot(code - 1, 16)
        moved[...] += lax.dot_general(
            spread(rows, mask), one_hot(slot_ref[0:1, at], CAP), NT, preferred_element_type=F32
        )
        return carry

    lax.fori_loop(0, v_ref.shape[1] // tile, step, 0)

    contacts = who_ref.shape[1]
    chunk = min(512, contacts)
    groups = seen.shape[1]
    sums = jnp.zeros((8 * 16, units), F32)
    parts = [halves(seen[k]) for k in range(3)]
    book = jnp.concatenate([jnp.concatenate(p, axis=1) for p in parts], axis=0)
    for c in range(contacts // chunk):
        at = slice(c * chunk, (c + 1) * chunk)
        hi, lo = split_index(who_ref[0:1, at], 128)
        hot = one_hot(lo, 128)
        got = jnp.dot(book, jnp.concatenate([hot, hot], axis=0), preferred_element_type=F32)
        here = lax.broadcasted_iota(jnp.int32, (groups, chunk), 0) == hi
        weight = weight_ref[0:1, at]
        rows = []
        for k in range(3):
            mine = jnp.where(here, got[k * groups : (k + 1) * groups], 0.0)
            rows.extend(halves(weight * jnp.sum(mine, axis=0, keepdims=True)))
        rows.extend(halves(weight))
        code, member = split_index(place_ref[0:1, at], units)
        sums = sums + lax.dot_general(
            spread(rows, one_hot(code, 16)), one_hot(member, units), NT, preferred_element_type=F32
        )
    totals = [sums[32 * k : 32 * k + 16] + sums[32 * k + 16 : 32 * k + 32] for k in range(4)]
    own_ref[...] = jnp.concatenate([t[6:7] for t in totals], axis=0)
    for d, out in enumerate((o0, o1, o2, o3, o4, o5)):
        out[...] = jnp.zeros_like(out)
        for k in range(3):
            out[k : k + 1, 0:CAP] = (
                moved[32 * k + d : 32 * k + d + 1] + moved[32 * k + 16 + d : 32 * k + 17 + d]
            )
        for k in range(4):
            out[4 + k : 5 + k, 0:units] = totals[k][d : d + 1]


def ring(axis, sign):
    count = lax.axis_size(axis)
    return [(i, (i + sign) % count) for i in range(count)]


def take(x, dim, where):
    start = x.shape[dim] - 1 if where < 0 else 0
    return lax.slice_in_dim(x, start, start + 1, axis=dim)


def pulled(x, dim, face, sign):
    size = x.shape[dim]
    if sign > 0:
        return jnp.concatenate([lax.slice_in_dim(x, 1, size, axis=dim), face], axis=dim)
    return jnp.concatenate([face, lax.slice_in_dim(x, 0, size - 1, axis=dim)], axis=dim)


def axis_tables(axis_index, grid_shift):
    first, second = axis_index[0], axis_index[1]
    for dim, axis in enumerate(("gx", "gy", "gz")):
        up = grid_shift[0, dim] > 0
        plus, minus = jnp.where(up, first, second), jnp.where(up, second, first)
        after = lax.ppermute(take(plus, dim, 0), axis, ring(axis, -1))
        before = lax.ppermute(take(minus, dim, -1), axis, ring(axis, 1))
        plus, minus = pulled(plus, dim, after, 1), pulled(minus, dim, before, -1)
        first, second = jnp.where(up, plus, minus), jnp.where(up, minus, plus)
    return first, second


def placed_mean(mean, shift):
    for dim, axis in enumerate(("gx", "gy", "gz")):
        d = dim + 1
        after = lax.ppermute(take(mean, d, 0), axis, ring(axis, -1))
        before = lax.ppermute(take(mean, d, -1), axis, ring(axis, 1))
        mean = jnp.where(shift[dim] > 0, pulled(mean, d, before, -1), pulled(mean, d, after, 1))
    return mean


def contact_places(contact_colloid, units):
    size_x, size_y, size_z = (lax.axis_size(a) for a in ("gx", "gy", "gz"))
    mine_x, mine_y, mine_z = (lax.axis_index(a) for a in ("gx", "gy", "gz"))
    owner = contact_colloid // units
    apart_x = (owner // (size_y * size_z) - mine_x) % size_x
    apart_y = (owner // size_z % size_y - mine_y) % size_y
    apart_z = (owner % size_z - mine_z) % size_z
    code = jnp.full(owner.shape, 6, jnp.int32)
    for number, (apart, to) in reversed(
        list(
            enumerate(
                (
                    (apart_x, 1), (apart_x, size_x - 1), (apart_y, 1),
                    (apart_y, size_y - 1), (apart_z, 1), (apart_z, size_z - 1),
                )
            )
        )
    ):
        code = jnp.where(apart == to, number, code)
    return code * units + contact_colloid % units


def body(
    velocities, particle_cells, grid_shift, axis_index, migrate_dir, migrate_slot,
    contact_colloid, contact_particle, contact_weight, colloid_velocity,
):
    _, cx, cy, nlo = axis_index.shape
    nhi = cx * cy
    particles = velocities.shape[1]
    units = colloid_velocity.shape[1]
    tile = math.gcd(particles, TILE)
    mean_shape = jax.ShapeDtypeStruct((3, nhi, nlo), F32)
    acc = pltpu.VMEM((7 * nhi, nlo), F32)
    table = pltpu.VMEM((4 * nhi, 2 * nlo), BF)
    params = pltpu.CompilerParams(vmem_limit_bytes=48 * 2**20)
    vmem = pl.BlockSpec(memory_space=pltpu.VMEM)

    def call(kernel, outs, scratch, flops, *args):
        many = isinstance(outs, tuple)
        return pl.pallas_call(
            functools.partial(kernel, tile, nhi, nlo),
            out_shape=outs,
            in_specs=[vmem] * len(args),
            out_specs=tuple([vmem] * len(outs)) if many else vmem,
            scratch_shapes=scratch,
            compiler_params=params,
            cost_estimate=pl.CostEstimate(flops=flops, bytes_accessed=30_000_000, transcendentals=0),
        )(*args)

    places = contact_places(contact_colloid, units)
    axis0, axis1 = axis_tables(axis_index, grid_shift)
    mean0 = call(first_kernel, mean_shape, [acc], 10**9, particle_cells, velocities)
    v1, mean1 = call(
        middle_kernel, (jax.ShapeDtypeStruct(velocities.shape, F32), mean_shape), [acc, table], 10**9,
        particle_cells, velocities, mean0, axis0.reshape(nhi, nlo),
    )
    box = jax.ShapeDtypeStruct((8, max(units, 256)), F32)
    outs = call(
        lambda t, h, l, *refs: last_kernel(t, h, l, units, *refs),
        (jax.ShapeDtypeStruct((3, particles + 6 * CAP), F32),)
        + (box,) * 6
        + (jax.ShapeDtypeStruct((4, units), F32),),
        [pltpu.VMEM((96, CAP), F32), table, pltpu.VMEM((3, particles // 128, 128), F32)],
        10**9,
        particle_cells, v1, mean1, axis1.reshape(nhi, nlo), migrate_dir.reshape(1, -1),
        migrate_slot.reshape(1, -1), places.reshape(1, -1), contact_particle.reshape(1, -1),
        contact_weight.reshape(1, -1),
    )
    cell_velocity = placed_mean(mean1.reshape(3, cx, cy, nlo), grid_shift[axis_index.shape[0] - 1])
    arrived = [
        lax.ppermute(outs[1 + d], ("gx", "gy", "gz")[d // 2], ring(("gx", "gy", "gz")[d // 2], 1 - 2 * (d % 2)))
        for d in range(6)
    ]
    tail = jnp.concatenate([a[0:3, 0:CAP] for a in arrived], axis=1)
    migrated = lax.dynamic_update_slice(outs[0], tail, (0, particles))
    total = outs[7]
    for a in arrived:
        total = total + a[4:8, 0:units]
    sum_w = total[3:4]
    force = (total[0:3] - sum_w * colloid_velocity) / jnp.maximum(sum_w, 1.0)
    return (cell_velocity, migrated, force)


def solution(mesh):
    flat = P(None, ("gx", "gy", "gz"))
    line = P(("gx", "gy", "gz"))
    grid = P(None, "gx", "gy", "gz")
    return jax.shard_map(
        body,
        mesh=mesh,
        in_specs=(flat, flat, P(), grid, line, line, line, line, line, flat),
        out_specs=(grid, flat, flat),
        check_vma=False,
    )
```

time: 1530 us -> 93.4 us (0.06)
  other arithmetic: 929 us -> 2.26 us
  local copies, waits for them, and re-layouts: 470 us -> 6.73 us
  starting transfers between devices: 81.8 us -> 23 us
  Pallas kernels: 0 us -> 44.4 us
  waiting for transfers between devices: 39.4 us -> 11.7 us
    scatter-add x6 -> x0, other arithmetic: 903 us -> none  [the longest x2 439 us: body(): momentum = jnp.zeros((3, extent_total), jnp.float32).at[:, wide_cell].add...]
    gather x4 -> x0, local copies, waits for them, and re-layouts: 297 us -> none  [body(): picked = reach[:, wide_cell]]
    scatter x19 -> x0, local copies, waits for them, and re-layouts: 101 us -> none  [the longest x1 100 us: body(): blocks = jnp.zeros((3, 6 * CAP), jnp.float32).at[:, target].set(velocity_...]
    ppermute x54 -> x18, starting transfers between devices: 81.8 us -> 23 us  [the longest x6 7.71 us: body(): lax.ppermute(outs[1 + d], ('gx', 'gy', 'gz')[d // 2], ring(('gx', 'gy', '...]
    pallas_call x0 -> x3, Pallas kernels: none -> 44.4 us  [call(): pl.pallas_call(functools.partial(kernel, tile, nhi, nlo), out_shape=outs,...]
    add x3 -> x0, local copies, waits for them, and re-layouts: 30.1 us -> none  [body(): velocity_now = apply_rotation(picked[:9], velocity_now) + picked[9:]]
    ppermute x54 -> x18, waiting for transfers between devices: 39.4 us -> 11.7 us  [the longest x3 5.7 us: axis_tables(): before = lax.ppermute(take(minus, dim, -1), axis, ring(axis, 1))]
  transfers between devices with their start and end apart: 54 -> 18, of which waited for: 23 -> 6; matrix products, arithmetic and copies ran while one was open for 31% -> 2% of each run, Pallas kernels for 0% -> 9%
where the time goes in v1:
time: 93.4 us; the launch traced here: 92.8 us
  Pallas kernels  44.4 us (48%)
  starting transfers between devices  23 us (25%)
  waiting for transfers between devices  11.7 us (13%)
  local copies, waits for them, and re-layouts  6.73 us (7%)
  between operations  4.68 us (5%)
  other arithmetic  2.26 us (2%)
    pallas_call x3, Pallas kernels, call(): pl.pallas_call(functools.partial(kernel, tile, nhi, nlo), out_shape=outs,...  44.4 us
    ppermute x6, starting transfers between devices, body(): lax.ppermute(outs[1 + d], ('gx', 'gy', 'gz')[d // 2], ring(('gx', 'gy', '...  7.71 us
    ppermute x3, starting transfers between devices, placed_mean(): after = lax.ppermute(take(mean, d, 0), axis, ring(axis, -1))  7.02 us
    ppermute x3, waiting for transfers between devices, axis_tables(): before = lax.ppermute(take(minus, dim, -1), axis, ring(axis, 1))  5.7 us
    ppermute x3, starting transfers between devices, axis_tables(): after = lax.ppermute(take(plus, dim, 0), axis, ring(axis, -1))  5.67 us
    unnamed x16, local copies, waits for them, and re-layouts  4.11 us
    ppermute x3, waiting for transfers between devices, placed_mean(): before = lax.ppermute(take(mean, d, -1), axis, ring(axis, 1))  3.29 us
    ppermute x3, starting transfers between devices, axis_tables(): before = lax.ppermute(take(minus, dim, -1), axis, ring(axis, 1))  2 us
  transfers between devices with their start and end apart: 18, of which 6 were waited for; matrix products, arithmetic and copies ran while one was open for 2% of the time, Pallas kernels for 9%

profile of v1, /device:TPU:0, one launch (start us, length us, event | category | flops | bytes accessed | tf_op | source)
XLA Modules:
  0.0 92.8 jit_solution(2761855136685377529)
XLA Ops:
  0.6 1.6 %fusion.29 = (s32[1,1]{1,0:T(1,128)}, s32[1,1]{1,0:T(1,128)}, s32[1,1]{1,0:T(1,128)}, s32[1,1]{1,0:T(1,128)}, s32[1,1]{1,0:T(1,128)}, /*index=5*/s32[1,1]{1,0:T(1,128)}) fusion(s32[2,3]{1,0:T(2,128)} %param.12), kind=kLoop, calls=%fused_computation.89 | loop fusion | bytes 48 | tf_op jit(solution)/shard_map/slice | solution.py:225
  2.8 0.7 slice_select_fusion.1
  3.6 5.1 %collective-permute-start = (s32[1,8,128]{2,1,0:T(8,128)S(1)}, s32[1,8,128]{2,1,0:T(8,128)S(1)}, u32[]{:S(2)}, u32[]{:S(2)}) collective-permute-start(s32[1,8,128]{2,1,0:T(8,128)S(1)} %slice_bitcast_fusion.5), channel_id=1, source_target_pairs={{0,24},{8,0},{16,8},{24,16},{1,25},{9,1},{17,9},{25,17},{2,26},{10... | collective-permute-start | bytes 12296 | tf_op jit(solution)/shard_map/ppermute | solution.py:213
  8.6 0.0 collective-permute-start.1
  8.7 0.0 copy-start.6
  8.7 0.7 copy-done.6
  10.0 0.0 collective-permute-done
  10.0 4.1 %collective-permute-done.1 = s32[1,8,128]{2,1,0:T(8,128)S(1)} collective-permute-done((s32[1,8,128]{2,1,0:T(8,128)S(1)}, s32[1,8,128]{2,1,0:T(8,128)S(1)}, u32[]{:S(2)}, u32[]{:S(2)}) %collective-permute-start.1) | collective-permute-done | bytes 4128 | tf_op jit(solution)/shard_map/ppermute | solution.py:214
  14.1 0.1 collective-permute-start.2
  14.1 0.5 collective-permute-start.3
  14.6 0.0 copy-start
  14.6 1.1 %copy-done = f32[3,40960]{1,0:T(4,128)S(1)} copy-done((f32[3,40960]{1,0:T(4,128)S(1)}, f32[3,40960]{1,0:T(4,128)}, u32[]{:S(2)}) %copy-start) | copy-done | bytes 491544
  15.7 0.0 copy-start.1
  15.7 1.0 %copy-done.1 = s32[2,40960]{1,0:T(2,128)S(1)} copy-done((s32[2,40960]{1,0:T(2,128)S(1)}, s32[2,40960]{1,0:T(2,128)}, u32[]{:S(2)}) %copy-start.1) | copy-done | bytes 327704
  16.7 8.6 %shard_map.121.mean_ref = f32[3,32,128]{2,1,0:T(8,128)S(1)} custom-call(s32[2,40960]{1,0:T(2,128)S(1)} %copy-done.1, f32[3,40960]{1,0:T(4,128)S(1)} %copy-done), custom_call_target="tpu_custom_call" | custom-call | flops 1000000000 | bytes 30000000 | tf_op jit(solution)/shard_map/pallas_call | solution.py:268
  27.9 0.0 collective-permute-done.2
  27.9 0.0 collective-permute-done.3
  27.9 0.1 slice.217
  28.0 1.5 %collective-permute-start.5 = (s32[4,8,1]{2,1,0:T(8,128)S(1)}, s32[4,8,1]{2,1,0:T(8,128)S(1)}, u32[]{:S(2)}, u32[]{:S(2)}) collective-permute-start(s32[4,8,1]{2,1,0:T(8,128)S(1)} %slice.217), channel_id=1, source_target_pairs={{0,1},{1,0},{2,3},{3,2},{4,5},{5,4},{6,7},{7,6},{8,9},{9,8},{10,11... | collective-permute-start | bytes 392 | tf_op jit(solution)/shard_map/ppermute | solution.py:214
  29.5 0.5 collective-permute-start.4
  30.0 0.1 slice_bitcast_fusion.1
  30.1 1.6 %collective-permute-done.5 = s32[4,8,1]{2,1,0:T(8,128)S(1)} collective-permute-done((s32[4,8,1]{2,1,0:T(8,128)S(1)}, s32[4,8,1]{2,1,0:T(8,128)S(1)}, u32[]{:S(2)}, u32[]{:S(2)}) %collective-permute-start.5) | collective-permute-done | bytes 160 | tf_op jit(solution)/shard_map/ppermute | solution.py:214
  31.8 1.6 %collective-permute-done.4 = s32[4,8,1]{2,1,0:T(8,128)S(1)} collective-permute-done((s32[4,8,1]{2,1,0:T(8,128)S(1)}, s32[4,8,1]{2,1,0:T(8,128)S(1)}, u32[]{:S(2)}, u32[]{:S(2)}) %collective-permute-start.4) | collective-permute-done | bytes 160 | tf_op jit(solution)/shard_map/ppermute | solution.py:213
  33.4 0.1 broadcast_select_fusion.4
  33.5 0.0 copy-start.5
  33.5 17.7 %shard_map.122 = (f32[3,40960]{1,0:T(4,128)S(1)}, f32[3,32,128]{2,1,0:T(8,128)S(1)}) custom-call(s32[2,40960]{1,0:T(2,128)S(1)} %copy-done.1, f32[3,40960]{1,0:T(4,128)S(1)} %copy-done, f32[3,32,128]{2,1,0:T(8,128)S(1)} %shard_map.121.mean_ref, s32[32,128]{1,0:T(8,128)S(1)} %get-tuple-element.24.axis_ref), custom_call_target="tpu_custom_call" | custom-call | flops 1000000000 | bytes 30000000 | tf_op jit(solution)/shard_map/pallas_call | solution.py:268
  51.1 0.0 copy-start.4
  51.1 0.0 copy-done.2
  51.2 0.0 copy-done.3
  51.2 0.0 copy-done.5
  51.2 0.7 copy-done.4
  51.8 18.1 %shard_map.123 = (f32[3,41920]{1,0:T(4,128)}, f32[8,256]{1,0:T(8,128)S(1)}, f32[8,256]{1,0:T(8,128)S(1)}, f32[8,256]{1,0:T(8,128)S(1)}, f32[8,256]{1,0:T(8,128)S...) custom-call(s32[2,40960]{1,0:T(2,128)S(1)} %copy-done.1, ...), custom_call_target="tpu_custom_call" | custom-call | flops 1000000000 | bytes 30000000 | tf_op jit(solution)/shard_map/pallas_call | solution.py:268
  70.0 0.1 collective-permute-start.12
  70.0 3.8 %collective-permute-start.13 = (f32[8,256]{1,0:T(8,128)S(1)}, f32[8,256]{1,0:T(8,128)S(1)}, u32[]{:S(2)}, u32[]{:S(2)}) collective-permute-start(f32[8,256]{1,0:T(8,128)S(1)} %get-tuple-element.17), channel_id=1, source_target_pairs={{0,24},{8,0},{16,8},{24,16},{1,25},{9,1},{17,9},{25,17},{2,26},{10... | collective-permute-start | bytes 24584 | tf_op jit(solution)/shard_map/ppermute | solution.py:299
  73.9 0.0 collective-permute-start.14
  73.9 1.7 %collective-permute-start.15 = (f32[8,256]{1,0:T(8,128)S(1)}, f32[8,256]{1,0:T(8,128)S(1)}, u32[]{:S(2)}, u32[]{:S(2)}) collective-permute-start(f32[8,256]{1,0:T(8,128)S(1)} %get-tuple-element.19), channel_id=1, source_target_pairs={{0,6},{2,0},{4,2},{6,4},{1,7},{3,1},{5,3},{7,5},{8,14},{10,8},{12,... | collective-permute-start | bytes 24584 | tf_op jit(solution)/shard_map/ppermute | solution.py:299
  75.6 0.5 collective-permute-start.16
  76.2 0.0 collective-permute-done.12
  76.2 1.5 %collective-permute-start.17 = (f32[8,256]{1,0:T(8,128)S(1)}, f32[8,256]{1,0:T(8,128)S(1)}, u32[]{:S(2)}, u32[]{:S(2)}) collective-permute-start(f32[8,256]{1,0:T(8,128)S(1)} %get-tuple-element.21), channel_id=1, source_target_pairs={{0,1},{1,0},{2,3},{3,2},{4,5},{5,4},{6,7},{7,6},{8,9},{9,8},{10,11... | collective-permute-start | bytes 24584 | tf_op jit(solution)/shard_map/ppermute | solution.py:299
  77.7 0.0 collective-permute-done.13
  77.7 0.0 collective-permute-start.6
  77.7 0.0 collective-permute-done.14
  77.7 3.8 %collective-permute-start.7 = (f32[3,1,8,128]{3,2,1,0:T(8,128)S(1)}, f32[3,1,8,128]{3,2,1,0:T(8,128)S(1)}, u32[]{:S(2)}, u32[]{:S(2)}) collective-permute-start(f32[3,1,8,128]{3,2,1,0:T(8,128)S(1)} %get-tuple-element.35), channel_id=1, source_target_pairs={{0,24},{8,0},{16,8},{24,16},{1,25},{9,1},{17,9},{25,17},{2,26},{10... | collective-permute-start | bytes 36872 | tf_op jit(solution)/shard_map/ppermute | solution.py:223
  81.5 0.0 collective-permute-done.15
  81.5 0.0 collective-permute-done.16
  81.5 0.0 collective-permute-done.17
  81.6 0.0 copy-start.7
  81.6 0.7 copy-done.7
  82.3 0.6 fusion.21
  82.9 0.1 concatenate.67
  83.0 0.6 constant_dynamic-update-slice_fusion
  83.6 0.0 collective-permute-done.6
  83.6 0.0 collective-permute-done.7
  83.7 0.1 collective-permute-start.8
  83.7 1.7 %collective-permute-start.9 = (f32[3,4,1,128]{3,2,1,0:T(1,128)S(1)}, f32[3,4,1,128]{3,2,1,0:T(1,128)S(1)}, u32[]{:S(2)}, u32[]{:S(2)}) collective-permute-start(f32[3,4,1,128]{3,2,1,0:T(1,128)S(1)} %get-tuple-element.31), channel_id=1, source_target_pairs={{0,6},{2,0},{4,2},{6,4},{1,7},{3,1},{5,3},{7,5},{8,14},{10,8},{12,... | collective-permute-start | bytes 18440 | tf_op jit(solution)/shard_map/ppermute | solution.py:223
  85.5 1.3 %collective-permute-done.8 = f32[3,4,1,128]{3,2,1,0:T(1,128)S(1)} collective-permute-done((f32[3,4,1,128]{3,2,1,0:T(1,128)S(1)}, f32[3,4,1,128]{3,2,1,0:T(1,128)S(1)}, u32[]{:S(2)}, u32[]{:S(2)}) %collective-permute-start.8) | collective-permute-done | bytes 6176 | tf_op jit(solution)/shard_map/ppermute | solution.py:224
  86.8 0.0 collective-permute-done.9
  86.8 0.1 fusion.23
  86.9 0.6 collective-permute-start.10
  87.5 1.5 %collective-permute-start.11 = (f32[3,4,8,1]{3,2,1,0:T(8,128)S(1)}, f32[3,4,8,1]{3,2,1,0:T(8,128)S(1)}, u32[]{:S(2)}, u32[]{:S(2)}) collective-permute-start(f32[3,4,8,1]{3,2,1,0:T(8,128)S(1)} %get-tuple-element.27), channel_id=1, source_target_pairs={{0,1},{1,0},{2,3},{3,2},{4,5},{5,4},{6,7},{7,6},{8,9},{9,8},{10,11... | collective-permute-start | bytes 1160 | tf_op jit(solution)/shard_map/ppermute | solution.py:223
  89.0 0.1 fusion.22
  89.0 2.0 %collective-permute-done.10 = f32[3,4,8,1]{3,2,1,0:T(8,128)S(1)} collective-permute-done((f32[3,4,8,1]{3,2,1,0:T(8,128)S(1)}, f32[3,4,8,1]{3,2,1,0:T(8,128)S(1)}, u32[]{:S(2)}, u32[]{:S(2)}) %collective-permute-start.10) | collective-permute-done | bytes 416 | tf_op jit(solution)/shard_map/ppermute | solution.py:224
  91.0 1.1 %collective-permute-done.11 = f32[3,4,8,1]{3,2,1,0:T(8,128)S(1)} collective-permute-done((f32[3,4,8,1]{3,2,1,0:T(8,128)S(1)}, f32[3,4,8,1]{3,2,1,0:T(8,128)S(1)}, u32[]{:S(2)}, u32[]{:S(2)}) %collective-permute-start.11) | collective-permute-done | bytes 416 | tf_op jit(solution)/shard_map/ppermute | solution.py:223
  92.1 0.7 maximum_select_fusion.2
  (26 shorter events, 0.2 us)
Async XLA Ops:
  3.6 6.4 %collective-permute-start = (s32[1,8,128]{2,1,0:T(8,128)S(1)}, s32[1,8,128]{2,1,0:T(8,128)S(1)}, u32[]{:S(2)}, u32[]{:S(2)}) collective-permute-start(s32[1,8,128]{2,1,0:T(8,128)S(1)} %slice_bitcast_fusion.5), channel_id=1, source_target_pairs={{0,24},{8,0},{16,8},{24,16},{1,25},{9,1},{17,9},{25,17},{2,26},{10... | collective-permute-start | bytes 12296 | tf_op jit(solution)/shard_map/ppermute | solution.py:213
  8.6 5.4 %collective-permute-start.1 = (s32[1,8,128]{2,1,0:T(8,128)S(1)}, s32[1,8,128]{2,1,0:T(8,128)S(1)}, u32[]{:S(2)}, u32[]{:S(2)}) collective-permute-start(s32[1,8,128]{2,1,0:T(8,128)S(1)} %slice_bitcast_fusion.4), channel_id=1, source_target_pairs={{0,8},{8,16},{16,24},{24,0},{1,9},{9,17},{17,25},{25,1},{2,10},{10... | collective-permute-start | bytes 12296 | tf_op jit(solution)/shard_map/ppermute | solution.py:214
  8.7 0.7 copy-start.6
  14.1 13.8 %collective-permute-start.2 = (s32[4,1,128]{2,1,0:T(1,128)S(1)}, s32[4,1,128]{2,1,0:T(1,128)S(1)}, u32[]{:S(2)}, u32[]{:S(2)}) collective-permute-start(s32[4,1,128]{2,1,0:T(1,128)S(1)} %slice.212), channel_id=1, source_target_pairs={{0,6},{2,0},{4,2},{6,4},{1,7},{3,1},{5,3},{7,5},{8,14},{10,8},{12,... | collective-permute-start | bytes 6152 | tf_op jit(solution)/shard_map/ppermute | solution.py:213
  14.1 13.8 %collective-permute-start.3 = (s32[4,1,128]{2,1,0:T(1,128)S(1)}, s32[4,1,128]{2,1,0:T(1,128)S(1)}, u32[]{:S(2)}, u32[]{:S(2)}) collective-permute-start(s32[4,1,128]{2,1,0:T(1,128)S(1)} %slice.213), channel_id=1, source_target_pairs={{0,2},{2,4},{4,6},{6,0},{1,3},{3,5},{5,7},{7,1},{8,10},{10,12},{12... | collective-permute-start | bytes 6152 | tf_op jit(solution)/shard_map/ppermute | solution.py:214
  14.6 1.1 %copy-start = (f32[3,40960]{1,0:T(4,128)S(1)}, f32[3,40960]{1,0:T(4,128)}, u32[]{:S(2)}) copy-start(f32[3,40960]{1,0:T(4,128)} %v_ref.3) | copy-start | bytes 1474564
  15.7 1.0 %copy-start.1 = (s32[2,40960]{1,0:T(2,128)S(1)}, s32[2,40960]{1,0:T(2,128)}, u32[]{:S(2)}) copy-start(s32[2,40960]{1,0:T(2,128)} %refs_0_.1) | copy-start | bytes 983044
  28.0 3.8 %collective-permute-start.5 = (s32[4,8,1]{2,1,0:T(8,128)S(1)}, s32[4,8,1]{2,1,0:T(8,128)S(1)}, u32[]{:S(2)}, u32[]{:S(2)}) collective-permute-start(s32[4,8,1]{2,1,0:T(8,128)S(1)} %slice.217), channel_id=1, source_target_pairs={{0,1},{1,0},{2,3},{3,2},{4,5},{5,4},{6,7},{7,6},{8,9},{9,8},{10,11... | collective-permute-start | bytes 392 | tf_op jit(solution)/shard_map/ppermute | solution.py:214
  29.5 3.9 %collective-permute-start.4 = (s32[4,8,1]{2,1,0:T(8,128)S(1)}, s32[4,8,1]{2,1,0:T(8,128)S(1)}, u32[]{:S(2)}, u32[]{:S(2)}) collective-permute-start(s32[4,8,1]{2,1,0:T(8,128)S(1)} %bitcast.38), channel_id=1, source_target_pairs={{0,1},{1,0},{2,3},{3,2},{4,5},{5,4},{6,7},{7,6},{8,9},{9,8},{10,11... | collective-permute-start | bytes 392 | tf_op jit(solution)/shard_map/ppermute | solution.py:213
  33.5 17.7 %copy-start.2 = (s32[40960]{0:T(1024)S(1)}, s32[40960]{0:T(1024)}, u32[]{:S(2)}) copy-start(s32[40960]{0:T(1024)} %param.14) | copy-start | bytes 491524
  33.5 17.7 %copy-start.3 = (s32[40960]{0:T(1024)S(1)}, s32[40960]{0:T(1024)}, u32[]{:S(2)}) copy-start(s32[40960]{0:T(1024)} %param.15) | copy-start | bytes 491524
  33.5 17.7 %copy-start.5 = (f32[2048]{0:T(1024)S(1)}, f32[2048]{0:T(1024)}, u32[]{:S(2)}) copy-start(f32[2048]{0:T(1024)} %param.18) | copy-start | bytes 24580
  51.1 0.7 copy-start.4
  70.0 6.2 %collective-permute-start.12 = (f32[8,256]{1,0:T(8,128)S(1)}, f32[8,256]{1,0:T(8,128)S(1)}, u32[]{:S(2)}, u32[]{:S(2)}) collective-permute-start(f32[8,256]{1,0:T(8,128)S(1)} %get-tuple-element.16), channel_id=1, source_target_pairs={{0,8},{8,16},{16,24},{24,0},{1,9},{9,17},{17,25},{25,1},{2,10},{10... | collective-permute-start | bytes 24584 | tf_op jit(solution)/shard_map/ppermute | solution.py:299
  70.0 7.7 %collective-permute-start.13 = (f32[8,256]{1,0:T(8,128)S(1)}, f32[8,256]{1,0:T(8,128)S(1)}, u32[]{:S(2)}, u32[]{:S(2)}) collective-permute-start(f32[8,256]{1,0:T(8,128)S(1)} %get-tuple-element.17), channel_id=1, source_target_pairs={{0,24},{8,0},{16,8},{24,16},{1,25},{9,1},{17,9},{25,17},{2,26},{10... | collective-permute-start | bytes 24584 | tf_op jit(solution)/shard_map/ppermute | solution.py:299
  73.9 3.9 %collective-permute-start.14 = (f32[8,256]{1,0:T(8,128)S(1)}, f32[8,256]{1,0:T(8,128)S(1)}, u32[]{:S(2)}, u32[]{:S(2)}) collective-permute-start(f32[8,256]{1,0:T(8,128)S(1)} %get-tuple-element.18), channel_id=1, source_target_pairs={{0,2},{2,4},{4,6},{6,0},{1,3},{3,5},{5,7},{7,1},{8,10},{10,12},{12... | collective-permute-start | bytes 24584 | tf_op jit(solution)/shard_map/ppermute | solution.py:299
  73.9 7.7 %collective-permute-start.15 = (f32[8,256]{1,0:T(8,128)S(1)}, f32[8,256]{1,0:T(8,128)S(1)}, u32[]{:S(2)}, u32[]{:S(2)}) collective-permute-start(f32[8,256]{1,0:T(8,128)S(1)} %get-tuple-element.19), channel_id=1, source_target_pairs={{0,6},{2,0},{4,2},{6,4},{1,7},{3,1},{5,3},{7,5},{8,14},{10,8},{12,... | collective-permute-start | bytes 24584 | tf_op jit(solution)/shard_map/ppermute | solution.py:299
  75.6 5.9 %collective-permute-start.16 = (f32[8,256]{1,0:T(8,128)S(1)}, f32[8,256]{1,0:T(8,128)S(1)}, u32[]{:S(2)}, u32[]{:S(2)}) collective-permute-start(f32[8,256]{1,0:T(8,128)S(1)} %get-tuple-element.20), channel_id=1, source_target_pairs={{0,1},{1,0},{2,3},{3,2},{4,5},{5,4},{6,7},{7,6},{8,9},{9,8},{10,11... | collective-permute-start | bytes 24584 | tf_op jit(solution)/shard_map/ppermute | solution.py:299
  76.2 5.4 %collective-permute-start.17 = (f32[8,256]{1,0:T(8,128)S(1)}, f32[8,256]{1,0:T(8,128)S(1)}, u32[]{:S(2)}, u32[]{:S(2)}) collective-permute-start(f32[8,256]{1,0:T(8,128)S(1)} %get-tuple-element.21), channel_id=1, source_target_pairs={{0,1},{1,0},{2,3},{3,2},{4,5},{5,4},{6,7},{7,6},{8,9},{9,8},{10,11... | collective-permute-start | bytes 24584 | tf_op jit(solution)/shard_map/ppermute | solution.py:299
  77.7 5.9 %collective-permute-start.6 = (f32[3,1,8,128]{3,2,1,0:T(8,128)S(1)}, f32[3,1,8,128]{3,2,1,0:T(8,128)S(1)}, u32[]{:S(2)}, u32[]{:S(2)}) collective-permute-start(f32[3,1,8,128]{3,2,1,0:T(8,128)S(1)} %get-tuple-element.36), channel_id=1, source_target_pairs={{0,8},{8,16},{16,24},{24,0},{1,9},{9,17},{17,25},{25,1},{2,10},{10... | collective-permute-start | bytes 36872 | tf_op jit(solution)/shard_map/ppermute | solution.py:224
  77.7 5.9 %collective-permute-start.7 = (f32[3,1,8,128]{3,2,1,0:T(8,128)S(1)}, f32[3,1,8,128]{3,2,1,0:T(8,128)S(1)}, u32[]{:S(2)}, u32[]{:S(2)}) collective-permute-start(f32[3,1,8,128]{3,2,1,0:T(8,128)S(1)} %get-tuple-element.35), channel_id=1, source_target_pairs={{0,24},{8,0},{16,8},{24,16},{1,25},{9,1},{17,9},{25,17},{2,26},{10... | collective-permute-start | bytes 36872 | tf_op jit(solution)/shard_map/ppermute | solution.py:223
  81.6 0.7 copy-start.7
  83.7 3.1 %collective-permute-start.8 = (f32[3,4,1,128]{3,2,1,0:T(1,128)S(1)}, f32[3,4,1,128]{3,2,1,0:T(1,128)S(1)}, u32[]{:S(2)}, u32[]{:S(2)}) collective-permute-start(f32[3,4,1,128]{3,2,1,0:T(1,128)S(1)} %get-tuple-element.32), channel_id=1, source_target_pairs={{0,2},{2,4},{4,6},{6,0},{1,3},{3,5},{5,7},{7,1},{8,10},{10,12},{12... | collective-permute-start | bytes 18440 | tf_op jit(solution)/shard_map/ppermute | solution.py:224
  83.7 3.1 %collective-permute-start.9 = (f32[3,4,1,128]{3,2,1,0:T(1,128)S(1)}, f32[3,4,1,128]{3,2,1,0:T(1,128)S(1)}, u32[]{:S(2)}, u32[]{:S(2)}) collective-permute-start(f32[3,4,1,128]{3,2,1,0:T(1,128)S(1)} %get-tuple-element.31), channel_id=1, source_target_pairs={{0,6},{2,0},{4,2},{6,4},{1,7},{3,1},{5,3},{7,5},{8,14},{10,8},{12,... | collective-permute-start | bytes 18440 | tf_op jit(solution)/shard_map/ppermute | solution.py:223
  86.9 4.1 %collective-permute-start.10 = (f32[3,4,8,1]{3,2,1,0:T(8,128)S(1)}, f32[3,4,8,1]{3,2,1,0:T(8,128)S(1)}, u32[]{:S(2)}, u32[]{:S(2)}) collective-permute-start(f32[3,4,8,1]{3,2,1,0:T(8,128)S(1)} %get-tuple-element.28), channel_id=1, source_target_pairs={{0,1},{1,0},{2,3},{3,2},{4,5},{5,4},{6,7},{7,6},{8,9},{9,8},{10,11... | collective-permute-start | bytes 1160 | tf_op jit(solution)/shard_map/ppermute | solution.py:224
  87.5 4.6 %collective-permute-start.11 = (f32[3,4,8,1]{3,2,1,0:T(8,128)S(1)}, f32[3,4,8,1]{3,2,1,0:T(8,128)S(1)}, u32[]{:S(2)}, u32[]{:S(2)}) collective-permute-start(f32[3,4,8,1]{3,2,1,0:T(8,128)S(1)} %get-tuple-element.27), channel_id=1, source_target_pairs={{0,1},{1,0},{2,3},{3,2},{4,5},{5,4},{6,7},{7,6},{8,9},{9,8},{10,11... | collective-permute-start | bytes 1160 | tf_op jit(solution)/shard_map/ppermute | solution.py:223

commit v2 on v1

--- a/solution.py
+++ b/solution.py
@@ -188,42 +188,114 @@
             out[4 + k : 5 + k, 0:units] = totals[k][d : d + 1]
 
 
-def ring(axis, sign):
+AXES = ("gx", "gy", "gz")
+MESH = pl.DeviceIdType.MESH
+
+
+def beside(axis, sign):
     count = lax.axis_size(axis)
-    return [(i, (i + sign) % count) for i in range(count)]
-
-
-def take(x, dim, where):
-    start = x.shape[dim] - 1 if where < 0 else 0
-    return lax.slice_in_dim(x, start, start + 1, axis=dim)
-
-
-def pulled(x, dim, face, sign):
-    size = x.shape[dim]
-    if sign > 0:
-        return jnp.concatenate([lax.slice_in_dim(x, 1, size, axis=dim), face], axis=dim)
-    return jnp.concatenate([face, lax.slice_in_dim(x, 0, size - 1, axis=dim)], axis=dim)
-
-
-def axis_tables(axis_index, grid_shift):
-    first, second = axis_index[0], axis_index[1]
-    for dim, axis in enumerate(("gx", "gy", "gz")):
-        up = grid_shift[0, dim] > 0
-        plus, minus = jnp.where(up, first, second), jnp.where(up, second, first)
-        after = lax.ppermute(take(plus, dim, 0), axis, ring(axis, -1))
-        before = lax.ppermute(take(minus, dim, -1), axis, ring(axis, 1))
-        plus, minus = pulled(plus, dim, after, 1), pulled(minus, dim, before, -1)
-        first, second = jnp.where(up, plus, minus), jnp.where(up, minus, plus)
-    return first, second
-
-
-def placed_mean(mean, shift):
-    for dim, axis in enumerate(("gx", "gy", "gz")):
-        d = dim + 1
-        after = lax.ppermute(take(mean, d, 0), axis, ring(axis, -1))
-        before = lax.ppermute(take(mean, d, -1), axis, ring(axis, 1))
-        mean = jnp.where(shift[dim] > 0, pulled(mean, d, before, -1), pulled(mean, d, after, 1))
-    return mean
+    return {axis: lax.rem(lax.axis_index(axis) + (sign + count), count)}
+
+
+def greet():
+    barrier = pltpu.get_barrier_semaphore()
+    for axis in AXES:
+        for sign in (1, -1):
+            pl.semaphore_signal(barrier, inc=1, device_id=beside(axis, sign), device_id_type=MESH)
+    pl.semaphore_wait(barrier, 6)
+
+
+def send(src, dst, sems, number, axis, sign):
+    copy = pltpu.make_async_remote_copy(
+        src_ref=src, dst_ref=dst, send_sem=sems[0].at[number], recv_sem=sems[1].at[number],
+        device_id=beside(axis, sign), device_id_type=MESH,
+    )
+    copy.start()
+    return copy
+
+
+def both(pair, box, sems, number, axis):
+    return [
+        send(pair[0], box.at[0], sems, number, axis, -1),
+        send(pair[1], box.at[1], sems, number + 1, axis, 1),
+    ]
+
+
+def shift_fields(rows, flip, shift_ref, x_ref, put, zbox, xbox, ybox, work, faces, sems, first):
+    n, cx, cy, nz = x_ref.shape
+    ups = [[shift_ref[r, dim] * flip > 0 for dim in range(3)] for r in rows]
+    for copy in both((x_ref, x_ref), zbox, sems, first, "gz"):
+        copy.wait()
+    for f in range(n):
+        x = x_ref[f]
+        plus = jnp.concatenate([x[:, :, 1:], zbox[0, f][:, :, 0:1]], axis=2)
+        minus = jnp.concatenate([zbox[1, f][:, :, nz - 1 :], x[:, :, : nz - 1]], axis=2)
+        work[f] = jnp.where(ups[f][2], plus, minus)
+    for copy in both((work.at[:, 0], work.at[:, cx - 1]), xbox, sems, first + 2, "gx"):
+        copy.wait()
+    held = []
+    for f in range(n):
+        x = work[f]
+        plus = [x[i] for i in range(1, cx)] + [xbox[0, f]]
+        minus = [xbox[1, f]] + [x[i] for i in range(cx - 1)]
+        held.append([jnp.where(ups[f][0], p, m) for p, m in zip(plus, minus)])
+        for i in range(cx):
+            faces[0, f, i : i + 1, :] = held[f][i][0:1]
+            faces[1, f, i : i + 1, :] = held[f][i][cy - 1 :]
+    for copy in both((faces.at[0], faces.at[1]), ybox, sems, first + 4, "gy"):
+        copy.wait()
+    for f in range(n):
+        for i in range(cx):
+            x = held[f][i]
+            plus = jnp.concatenate([x[1:], ybox[0, f, i : i + 1, :]], axis=0)
+            minus = jnp.concatenate([ybox[1, f, i : i + 1, :], x[: cy - 1]], axis=0)
+            put(f, i, jnp.where(ups[f][1], plus, minus))
+
+
+def shift_scratch(shape, kind):
+    n, cx, cy, nz = shape
+    return [
+        pltpu.VMEM((2, n, cx, cy, nz), kind), pltpu.VMEM((2, n, cy, nz), kind),
+        pltpu.VMEM((2, n, cx, nz), kind), pltpu.VMEM((n, cx, cy, nz), kind),
+        pltpu.VMEM((2, n, cx, nz), kind),
+    ]
+
+
+def axis_kernel(shift_ref, x_ref, out_ref, zbox, xbox, ybox, work, faces, out_sem, in_sem):
+    greet()
+
+    def put(f, i, value):
+        out_ref[f, i] = value
+
+    rows = list(range(x_ref.shape[0]))
+    shift_fields(
+        rows, 1, shift_ref, x_ref, put, zbox, xbox, ybox, work, faces, (out_sem, in_sem), 0
+    )
+
+
+def tail_kernel(
+    units, shift_ref, x_ref, b0, b1, b2, b3, b4, b5, own_ref, drift_ref, out_ref, tail_ref, force_ref,
+    zbox, xbox, ybox, work, faces, arrived, out_sem, in_sem
+):
+    greet()
+    sems = (out_sem, in_sem)
+    copies = [
+        send(b, arrived.at[d], sems, 6 + d, AXES[d // 2], 1 - 2 * (d % 2))
+        for d, b in enumerate((b0, b1, b2, b3, b4, b5))
+    ]
+
+    def put(f, i, value):
+        out_ref[f, i] = value
+
+    rows = [shift_ref.shape[0] - 1] * x_ref.shape[0]
+    shift_fields(rows, -1, shift_ref, x_ref, put, zbox, xbox, ybox, work, faces, sems, 0)
+    total = own_ref[...]
+    for d, copy in enumerate(copies):
+        copy.wait()
+        tail_ref[:, d * CAP : (d + 1) * CAP] = arrived[d, 0:3, 0:CAP]
+        total = total + arrived[d, 4:8, 0:units]
+    sum_w = total[3:4]
+    force_ref[...] = (total[0:3] - sum_w * drift_ref[...]) / jnp.maximum(sum_w, 1.0)
 
 
 def contact_places(contact_colloid, units):
@@ -276,7 +348,17 @@
         )(*args)
 
     places = contact_places(contact_colloid, units)
-    axis0, axis1 = axis_tables(axis_index, grid_shift)
+    smem = pl.BlockSpec(memory_space=pltpu.SMEM)
+    turned = pl.pallas_call(
+        axis_kernel,
+        out_shape=jax.ShapeDtypeStruct(axis_index.shape, jnp.int32),
+        in_specs=[smem, vmem],
+        out_specs=vmem,
+        scratch_shapes=shift_scratch(axis_index.shape, jnp.int32)
+        + [pltpu.SemaphoreType.DMA((6,)), pltpu.SemaphoreType.DMA((6,))],
+        compiler_params=pltpu.CompilerParams(collective_id=0, has_side_effects=True),
+    )(grid_shift, axis_index)
+    axis0, axis1 = turned[0], turned[1]
     mean0 = call(first_kernel, mean_shape, [acc], 10**9, particle_cells, velocities)
     v1, mean1 = call(
         middle_kernel, (jax.ShapeDtypeStruct(velocities.shape, F32), mean_shape), [acc, table], 10**9,
@@ -294,18 +376,22 @@
         migrate_slot.reshape(1, -1), places.reshape(1, -1), contact_particle.reshape(1, -1),
         contact_weight.reshape(1, -1),
     )
-    cell_velocity = placed_mean(mean1.reshape(3, cx, cy, nlo), grid_shift[axis_index.shape[0] - 1])
-    arrived = [
-        lax.ppermute(outs[1 + d], ("gx", "gy", "gz")[d // 2], ring(("gx", "gy", "gz")[d // 2], 1 - 2 * (d % 2)))
-        for d in range(6)
-    ]
-    tail = jnp.concatenate([a[0:3, 0:CAP] for a in arrived], axis=1)
+    mean_box = mean1.reshape(3, cx, cy, nlo)
+    cell_velocity, tail, force = pl.pallas_call(
+        functools.partial(tail_kernel, units),
+        out_shape=(
+            jax.ShapeDtypeStruct(mean_box.shape, F32),
+            jax.ShapeDtypeStruct((3, 6 * CAP), F32),
+            jax.ShapeDtypeStruct((3, units), F32),
+        ),
+        in_specs=[smem] + [vmem] * 9,
+        out_specs=(vmem, vmem, vmem),
+        scratch_shapes=shift_scratch(mean_box.shape, F32)
+        + [pltpu.VMEM((6,) + box.shape, F32)]
+        + [pltpu.SemaphoreType.DMA((12,)), pltpu.SemaphoreType.DMA((12,))],
+        compiler_params=pltpu.CompilerParams(collective_id=1, has_side_effects=True),
+    )(grid_shift, mean_box, *outs[1:8], colloid_velocity)
     migrated = lax.dynamic_update_slice(outs[0], tail, (0, particles))
-    total = outs[7]
-    for a in arrived:
-        total = total + a[4:8, 0:units]
-    sum_w = total[3:4]
-    force = (total[0:3] - sum_w * colloid_velocity) / jnp.maximum(sum_w, 1.0)
     return (cell_velocity, migrated, force)
 
 

time: 93.4 us -> 86.4 us (0.925); the launches traced: 92.8 us -> 84.8 us
  Pallas kernels: 44.4 us -> 72.9 us
  starting transfers between devices: 23 us -> 0 us
  waiting for transfers between devices: 11.7 us -> 0 us
  local copies, waits for them, and re-layouts: 6.73 us -> 11 us
  between operations: 4.68 us -> 0.78 us
  other arithmetic: 2.26 us -> 0.04 us
    pallas_call x0 -> x2, Pallas kernels: none -> 28.4 us  [the longest x1 15.2 us: body(): pl.pallas_call(axis_kernel, out_shape=jax.ShapeDtypeStruct(axis_index.sha...]
    ppermute x18 -> x0, starting transfers between devices: 23 us -> none  [the longest x6 7.71 us: body(): lax.ppermute(outs[1 + d], ('gx', 'gy', 'gz')[d // 2], ring(('gx', 'gy', '...]
    ppermute x18 -> x0, waiting for transfers between devices: 11.7 us -> none  [the longest x3 5.7 us: axis_tables(): before = lax.ppermute(take(minus, dim, -1), axis, ring(axis, 1))]
    unnamed x16 -> x34, local copies, waits for them, and re-layouts: 4.11 us -> 8.94 us
    slice x20 -> x0, local copies, waits for them, and re-layouts: 1.83 us -> none  [the longest x1 1.55 us: placed_mean(): shift[dim] > 0]
    select_n x7 -> x0, other arithmetic: 1.59 us -> none  [the longest x3 0.76 us: axis_tables(): plus, minus = (jnp.where(up, first, second), jnp.where(up, second, first))]
  transfers between devices with their start and end apart: 18 -> 0, of which waited for: 6 -> 0; matrix products, arithmetic and copies ran while one was open for 2% -> 0% of each run, Pallas kernels for 9% -> 0%
where the time goes in v2:
time: 86.4 us; the launch traced here: 84.8 us
  Pallas kernels  72.9 us (84%)
  local copies, waits for them, and re-layouts  11 us (13%)
    pallas_call x3, Pallas kernels, call(): pl.pallas_call(functools.partial(kernel, tile, nhi, nlo), out_shape=outs,...  44.5 us
    pallas_call x1, Pallas kernels, body(): pl.pallas_call(axis_kernel, out_shape=jax.ShapeDtypeStruct(axis_index.sha...  15.2 us
    pallas_call x1, Pallas kernels, body(): pl.pallas_call(functools.partial(tail_kernel, units), out_shape=(jax.Shap...  13.3 us
    unnamed x34, local copies, waits for them, and re-layouts  8.94 us

profile of v2, /device:TPU:0, one launch (start us, length us, event | category | flops | bytes accessed | tf_op | source)
XLA Modules:
  0.0 84.8 jit_solution(16318889588853754929)
XLA Ops:
  0.6 0.0 copy-start.14
  0.6 0.7 copy-done.14
  1.4 15.2 %shard_map.122 = s32[2,4,8,128]{3,2,1,0:T(8,128)} custom-call(s32[2,3]{1,0:T(2,128)} %shift_ref.3, s32[2,4,8,128]{3,2,1,0:T(8,128)} %x_ref.1), custom_call_target="tpu_custom_call" | custom-call | tf_op jit(solution)/shard_map/pallas_call | solution.py:352
  16.6 0.7 slice_bitcast_fusion
  17.3 0.0 copy-start.8
  17.3 1.1 %copy-done.8 = f32[3,40960]{1,0:T(4,128)S(1)} copy-done((f32[3,40960]{1,0:T(4,128)S(1)}, f32[3,40960]{1,0:T(4,128)}, u32[]{:S(2)}) %copy-start.8) | copy-done | bytes 491544
  18.4 0.0 copy-start.9
  18.4 1.0 %copy-done.9 = s32[2,40960]{1,0:T(2,128)S(1)} copy-done((s32[2,40960]{1,0:T(2,128)S(1)}, s32[2,40960]{1,0:T(2,128)}, u32[]{:S(2)}) %copy-start.9) | copy-done | bytes 327704
  19.4 8.6 %shard_map.121.mean_ref = f32[3,32,128]{2,1,0:T(8,128)S(1)} custom-call(s32[2,40960]{1,0:T(2,128)S(1)} %copy-done.9, f32[3,40960]{1,0:T(4,128)S(1)} %copy-done.8), custom_call_target="tpu_custom_call" | custom-call | flops 1000000000 | bytes 30000000 | tf_op jit(solution)/shard_map/pallas_call | solution.py:340
  28.0 0.0 copy-start.10
  28.0 0.0 copy-start.11
  28.0 0.0 copy-start.12
  28.0 0.0 copy-start.13
  28.0 17.7 %shard_map.123 = (f32[3,40960]{1,0:T(4,128)S(1)}, f32[3,32,128]{2,1,0:T(8,128)S(1)}) custom-call(s32[2,40960]{1,0:T(2,128)S(1)} %copy-done.9, f32[3,40960]{1,0:T(4,128)S(1)} %copy-done.8, f32[3,32,128]{2,1,0:T(8,128)S(1)} %shard_map.121.mean_ref, s32[32,128]{1,0:T(8,128)S(1)} %get-tuple-element.30.axis_ref), custom_call_target="tpu_custom_call" | custom-call | flops 1000000000 | bytes 30000000 | tf_op jit(solution)/shard_map/pallas_call | solution.py:340
  45.7 0.0 copy-start
  45.7 0.0 copy-done.10
  45.7 0.0 copy-done.11
  45.7 0.0 copy-done.12
  45.7 0.0 copy-done.13
  45.7 18.2 %shard_map.124 = (f32[3,41920]{1,0:T(4,128)}, f32[8,256]{1,0:T(8,128)S(1)}, f32[8,256]{1,0:T(8,128)S(1)}, f32[8,256]{1,0:T(8,128)S(1)}, f32[8,256]{1,0:T(8,128)S...) custom-call(s32[2,40960]{1,0:T(2,128)S(1)} %copy-done.9, ...), custom_call_target="tpu_custom_call" | custom-call | flops 1000000000 | bytes 30000000 | tf_op jit(solution)/shard_map/pallas_call | solution.py:340
  64.0 0.0 copy-done
  64.0 0.0 copy-start.1
  64.0 0.6 copy-done.1
  64.6 0.0 copy-start.2
  64.6 0.6 copy-done.2
  65.2 0.0 copy-start.3
  65.2 0.6 copy-done.3
  65.8 0.0 copy-start.4
  65.8 0.6 copy-done.4
  66.4 0.0 copy-start.5
  66.4 0.6 copy-done.5
  67.0 0.0 copy-start.6
  67.0 0.6 copy-done.6
  67.5 0.0 copy-start.7
  67.6 0.6 copy-done.7
  68.1 13.3 %shard_map.125 = (f32[3,4,8,128]{3,2,1,0:T(8,128)}, f32[3,960]{1,0:T(4,128)}, f32[3,256]{1,0:T(4,128)}) custom-call(s32[2,3]{1,0:T(2,128)} %shift_ref.3, f32[3,4,8,128]{3,2,1,0:T(8,128)} %bitcast.10, f32[8,256]{1,0:T(8,128)} %copy-done.1, f32[8,256]{1,0:T(8,128)} %copy-done.2, f32[8,256]{1,0:T(8,128)} %copy-done.3, f32[8,256]{1,0:T(8,128)} %copy-done.4, ...), custom_call_target="tpu_custom_call" | custom-call | tf_op jit(solution)/shard_map/pallas_call | solution.py:380
  81.4 1.3 %constant_dynamic-update-slice_fusion = f32[3,41920]{1,0:T(4,128)} fusion(f32[3,41920]{1,0:T(4,128)} %get-tuple-element.26, f32[3,960]{1,0:T(4,128)} %get-tuple-element.27), kind=kLoop, calls=%fused_computation.47 | loop fusion | bytes 32768 | tf_op jit(solution)/shard_map/dynamic_update_slice | solution.py:394
  82.7 0.0 copy-start.15
  82.7 1.4 %copy.16 = f32[3,4,8,128]{3,2,1,0:T(8,128)} copy(f32[3,4,8,128]{3,2,1,0:T(8,128)} %get-tuple-element.34) | data formatting | bytes 98304
  84.2 0.0 copy-done.15
  84.2 0.6 copy.17
  (1 shorter events, 0.0 us)
Async XLA Ops:
  0.6 0.7 copy-start.14
  17.3 1.1 %copy-start.8 = (f32[3,40960]{1,0:T(4,128)S(1)}, f32[3,40960]{1,0:T(4,128)}, u32[]{:S(2)}) copy-start(f32[3,40960]{1,0:T(4,128)} %v_ref.3) | copy-start | bytes 1474564
  18.4 1.0 %copy-start.9 = (s32[2,40960]{1,0:T(2,128)S(1)}, s32[2,40960]{1,0:T(2,128)}, u32[]{:S(2)}) copy-start(s32[2,40960]{1,0:T(2,128)} %refs_0_.1) | copy-start | bytes 983044
  28.0 17.7 %copy-start.10 = (s32[40960]{0:T(1024)S(1)}, s32[40960]{0:T(1024)}, u32[]{:S(2)}) copy-start(s32[40960]{0:T(1024)} %param.14) | copy-start | bytes 491524
  28.0 17.7 %copy-start.11 = (s32[40960]{0:T(1024)S(1)}, s32[40960]{0:T(1024)}, u32[]{:S(2)}) copy-start(s32[40960]{0:T(1024)} %param.15) | copy-start | bytes 491524
  28.0 17.7 %copy-start.12 = (s32[2048]{0:T(1024)S(1)}, s32[2048]{0:T(1024)}, u32[]{:S(2)}) copy-start(s32[2048]{0:T(1024)} %param.17) | copy-start | bytes 24580
  28.0 17.7 %copy-start.13 = (f32[2048]{0:T(1024)S(1)}, f32[2048]{0:T(1024)}, u32[]{:S(2)}) copy-start(f32[2048]{0:T(1024)} %param.18) | copy-start | bytes 24580
  45.7 18.3 %copy-start = (f32[3,32,128]{2,1,0:T(8,128)}, f32[3,32,128]{2,1,0:T(8,128)S(1)}, u32[]{:S(2)}) copy-start(f32[3,32,128]{2,1,0:T(8,128)S(1)} %get-tuple-element.16.refs_2_) | copy-start | bytes 147460
  64.0 0.6 copy-start.1
  64.6 0.6 copy-start.2
  65.2 0.6 copy-start.3
  65.8 0.6 copy-start.4
  66.4 0.6 copy-start.5
  67.0 0.6 copy-start.6
  67.5 0.6 copy-start.7
  82.7 1.4 %copy-start.15 = (f32[3,256]{1,0:T(4,128)S(1)}, f32[3,256]{1,0:T(4,128)}, u32[]{:S(2)}) copy-start(f32[3,256]{1,0:T(4,128)} %get-tuple-element.36) | copy-start | bytes 9220

commit v3 on v2

--- a/solution.py
+++ b/solution.py
@@ -24,8 +24,9 @@
 
 
 def one_hot(row, count):
-    wide = lax.broadcasted_iota(jnp.int32, (count, row.shape[1]), 0)
-    return jnp.where(wide == row, 1.0, 0.0).astype(BF)
+    kind = BF if count <= 256 else F32
+    wide = lax.broadcasted_iota(jnp.int32, (count, row.shape[1]), 0).astype(F32).astype(kind)
+    return jnp.where(wide == row.astype(F32).astype(kind), jnp.ones((), kind), jnp.zeros((), kind)).astype(BF)
 
 
 def halves(x):
@@ -97,15 +98,25 @@
     return [ref[k : k + 1, at] for k in range(3)]
 
 
-def first_kernel(tile, nhi, nlo, cell_ref, v_ref, mean_ref, acc):
+def first_kernel(
+    tile, nhi, nlo, shift_ref, x_ref, cell_ref, v_ref, mean_ref, axis0_ref, axis1_ref,
+    acc, zbox, xbox, ybox, work, turned, faces, out_sem, in_sem
+):
     acc[...] = jnp.zeros_like(acc)
+    cy = x_ref.shape[2]
+
+    def put(f, i, value):
+        (axis0_ref, axis1_ref)[f][i * cy : (i + 1) * cy, :] = value
 
     def step(t, carry):
         at = pl.ds(pl.multiple_of(t * tile, tile), tile)
         acc[...] += hist_tile(cell_ref[0:1, at], rows3(v_ref, at), nhi, nlo)
         return carry
 
-    lax.fori_loop(0, v_ref.shape[1] // tile, step, 0)
+    transfer = shift_fields(
+        (0, 1), 1, shift_ref, x_ref, put, zbox, xbox, ybox, work, turned, faces, (out_sem, in_sem)
+    )
+    beside_work(transfer, step, v_ref.shape[1] // tile)
     mean_of(acc, mean_ref, nhi)
 
 
@@ -128,8 +139,9 @@
 
 
 def last_kernel(
-    tile, nhi, nlo, units, cell_ref, v_ref, mean_ref, axis_ref, dir_ref, slot_ref, place_ref, who_ref,
-    weight_ref, kept_ref, o0, o1, o2, o3, o4, o5, own_ref, moved, table_ref, seen
+    tile, nhi, nlo, units, shift_ref, x_ref, cell_ref, v_ref, mean_ref, axis_ref, dir_ref, slot_ref,
+    place_ref, who_ref, weight_ref, drift_ref, out_ref, kept_ref, force_ref, moved, table_ref, seen,
+    going, coming, pushes, pulls, zbox, xbox, ybox, work, turned, faces, out_sem, in_sem
 ):
     moved[...] = jnp.zeros_like(moved)
     make_table(mean_ref, axis_ref, table_ref, nhi, nlo)
@@ -152,7 +164,24 @@
         )
         return carry
 
-    lax.fori_loop(0, v_ref.shape[1] // tile, step, 0)
+    def put(f, i, value):
+        out_ref[f, i] = value
+
+    sems = (out_sem, in_sem)
+    rows_of_shift = [shift_ref.shape[0] - 1] * x_ref.shape[0]
+    transfer = shift_fields(
+        rows_of_shift, -1, shift_ref, x_ref, put, zbox, xbox, ybox, work, turned, faces, sems
+    )
+    particles = v_ref.shape[1]
+    beside_work(transfer, step, particles // tile)
+    for d in range(6):
+        for k in range(3):
+            going[d, k : k + 1, :] = (
+                moved[32 * k + d : 32 * k + d + 1] + moved[32 * k + 16 + d : 32 * k + 17 + d]
+            )
+    copies = [
+        send(going.at[d], coming.at[d], sems, 6 + d, AXES[d // 2], 1 - 2 * (d % 2)) for d in range(6)
+    ]
 
     contacts = who_ref.shape[1]
     chunk = min(512, contacts)
@@ -177,15 +206,21 @@
             spread(rows, one_hot(code, 16)), one_hot(member, units), NT, preferred_element_type=F32
         )
     totals = [sums[32 * k : 32 * k + 16] + sums[32 * k + 16 : 32 * k + 32] for k in range(4)]
-    own_ref[...] = jnp.concatenate([t[6:7] for t in totals], axis=0)
-    for d, out in enumerate((o0, o1, o2, o3, o4, o5)):
-        out[...] = jnp.zeros_like(out)
-        for k in range(3):
-            out[k : k + 1, 0:CAP] = (
-                moved[32 * k + d : 32 * k + d + 1] + moved[32 * k + 16 + d : 32 * k + 17 + d]
-            )
+    total = jnp.concatenate([t[6:7] for t in totals], axis=0)
+    for d in range(6):
         for k in range(4):
-            out[4 + k : 5 + k, 0:units] = totals[k][d : d + 1]
+            pushes[d, k : k + 1, :] = totals[k][d : d + 1]
+    more = [
+        send(pushes.at[d], pulls.at[d], sems, 12 + d, AXES[d // 2], 1 - 2 * (d % 2)) for d in range(6)
+    ]
+    for d, copy in enumerate(copies):
+        copy.wait()
+        kept_ref[:, particles + d * CAP : particles + (d + 1) * CAP] = coming[d, 0:3]
+    for d, copy in enumerate(more):
+        copy.wait()
+        total = total + pulls[d]
+    sum_w = total[3:4]
+    force_ref[...] = (total[0:3] - sum_w * drift_ref[...]) / jnp.maximum(sum_w, 1.0)
 
 
 AXES = ("gx", "gy", "gz")
@@ -198,11 +233,11 @@
 
 
 def greet():
-    barrier = pltpu.get_barrier_semaphore()
     for axis in AXES:
         for sign in (1, -1):
-            pl.semaphore_signal(barrier, inc=1, device_id=beside(axis, sign), device_id_type=MESH)
-    pl.semaphore_wait(barrier, 6)
+            pl.semaphore_signal(
+                pltpu.get_barrier_semaphore(), inc=1, device_id=beside(axis, sign), device_id_type=MESH
+            )
 
 
 def send(src, dst, sems, number, axis, sign):
@@ -221,32 +256,40 @@
     ]
 
 
-def shift_fields(rows, flip, shift_ref, x_ref, put, zbox, xbox, ybox, work, faces, sems, first):
+def shift_fields(rows, flip, shift_ref, x_ref, put, zbox, xbox, ybox, work, turned, faces, sems):
     n, cx, cy, nz = x_ref.shape
     ups = [[shift_ref[r, dim] * flip > 0 for dim in range(3)] for r in rows]
-    for copy in both((x_ref, x_ref), zbox, sems, first, "gz"):
+    greet()
+    yield
+    pl.semaphore_wait(pltpu.get_barrier_semaphore(), 6)
+    copies = both((x_ref, x_ref), zbox, sems, 0, "gz")
+    yield
+    for copy in copies:
         copy.wait()
     for f in range(n):
         x = x_ref[f]
         plus = jnp.concatenate([x[:, :, 1:], zbox[0, f][:, :, 0:1]], axis=2)
         minus = jnp.concatenate([zbox[1, f][:, :, nz - 1 :], x[:, :, : nz - 1]], axis=2)
         work[f] = jnp.where(ups[f][2], plus, minus)
-    for copy in both((work.at[:, 0], work.at[:, cx - 1]), xbox, sems, first + 2, "gx"):
-        copy.wait()
-    held = []
-    for f in range(n):
-        x = work[f]
-        plus = [x[i] for i in range(1, cx)] + [xbox[0, f]]
-        minus = [xbox[1, f]] + [x[i] for i in range(cx - 1)]
-        held.append([jnp.where(ups[f][0], p, m) for p, m in zip(plus, minus)])
-        for i in range(cx):
-            faces[0, f, i : i + 1, :] = held[f][i][0:1]
-            faces[1, f, i : i + 1, :] = held[f][i][cy - 1 :]
-    for copy in both((faces.at[0], faces.at[1]), ybox, sems, first + 4, "gy"):
+    copies = both((work.at[:, 0], work.at[:, cx - 1]), xbox, sems, 2, "gx")
+    yield
+    for copy in copies:
         copy.wait()
     for f in range(n):
         for i in range(cx):
-            x = held[f][i]
+            plus = work[f, i + 1] if i + 1 < cx else xbox[0, f]
+            minus = work[f, i - 1] if i > 0 else xbox[1, f]
+            row = jnp.where(ups[f][0], plus, minus)
+            turned[f, i] = row
+            faces[0, f, i : i + 1, :] = row[0:1]
+            faces[1, f, i : i + 1, :] = row[cy - 1 :]
+    copies = both((faces.at[0], faces.at[1]), ybox, sems, 4, "gy")
+    yield
+    for copy in copies:
+        copy.wait()
+    for f in range(n):
+        for i in range(cx):
+            x = turned[f, i]
             plus = jnp.concatenate([x[1:], ybox[0, f, i : i + 1, :]], axis=0)
             minus = jnp.concatenate([ybox[1, f, i : i + 1, :], x[: cy - 1]], axis=0)
             put(f, i, jnp.where(ups[f][1], plus, minus))
@@ -257,45 +300,16 @@
     return [
         pltpu.VMEM((2, n, cx, cy, nz), kind), pltpu.VMEM((2, n, cy, nz), kind),
         pltpu.VMEM((2, n, cx, nz), kind), pltpu.VMEM((n, cx, cy, nz), kind),
-        pltpu.VMEM((2, n, cx, nz), kind),
+        pltpu.VMEM((n, cx, cy, nz), kind), pltpu.VMEM((2, n, cx, nz), kind),
     ]
 
 
-def axis_kernel(shift_ref, x_ref, out_ref, zbox, xbox, ybox, work, faces, out_sem, in_sem):
-    greet()
-
-    def put(f, i, value):
-        out_ref[f, i] = value
-
-    rows = list(range(x_ref.shape[0]))
-    shift_fields(
-        rows, 1, shift_ref, x_ref, put, zbox, xbox, ybox, work, faces, (out_sem, in_sem), 0
-    )
-
-
-def tail_kernel(
-    units, shift_ref, x_ref, b0, b1, b2, b3, b4, b5, own_ref, drift_ref, out_ref, tail_ref, force_ref,
-    zbox, xbox, ybox, work, faces, arrived, out_sem, in_sem
-):
-    greet()
-    sems = (out_sem, in_sem)
-    copies = [
-        send(b, arrived.at[d], sems, 6 + d, AXES[d // 2], 1 - 2 * (d % 2))
-        for d, b in enumerate((b0, b1, b2, b3, b4, b5))
-    ]
-
-    def put(f, i, value):
-        out_ref[f, i] = value
-
-    rows = [shift_ref.shape[0] - 1] * x_ref.shape[0]
-    shift_fields(rows, -1, shift_ref, x_ref, put, zbox, xbox, ybox, work, faces, sems, 0)
-    total = own_ref[...]
-    for d, copy in enumerate(copies):
-        copy.wait()
-        tail_ref[:, d * CAP : (d + 1) * CAP] = arrived[d, 0:3, 0:CAP]
-        total = total + arrived[d, 4:8, 0:units]
-    sum_w = total[3:4]
-    force_ref[...] = (total[0:3] - sum_w * drift_ref[...]) / jnp.maximum(sum_w, 1.0)
+def beside_work(transfer, step, tiles):
+    for part in range(4):
+        next(transfer)
+        lax.fori_loop(tiles * part // 4, tiles * (part + 1) // 4, step, 0)
+    for _ in transfer:
+        pass
 
 
 def contact_places(contact_colloid, units):
@@ -332,67 +346,54 @@
     mean_shape = jax.ShapeDtypeStruct((3, nhi, nlo), F32)
     acc = pltpu.VMEM((7 * nhi, nlo), F32)
     table = pltpu.VMEM((4 * nhi, 2 * nlo), BF)
-    params = pltpu.CompilerParams(vmem_limit_bytes=48 * 2**20)
     vmem = pl.BlockSpec(memory_space=pltpu.VMEM)
-
-    def call(kernel, outs, scratch, flops, *args):
-        many = isinstance(outs, tuple)
+    smem = pl.BlockSpec(memory_space=pltpu.SMEM)
+
+    def call(kernel, outs, scratch, number, *args):
+        extra = {} if number is None else dict(collective_id=number, has_side_effects=True)
+        first = vmem if number is None else smem
         return pl.pallas_call(
             functools.partial(kernel, tile, nhi, nlo),
             out_shape=outs,
-            in_specs=[vmem] * len(args),
-            out_specs=tuple([vmem] * len(outs)) if many else vmem,
+            in_specs=[first] + [vmem] * (len(args) - 1),
+            out_specs=tuple([vmem] * len(outs)),
             scratch_shapes=scratch,
-            compiler_params=params,
-            cost_estimate=pl.CostEstimate(flops=flops, bytes_accessed=30_000_000, transcendentals=0),
+            compiler_params=pltpu.CompilerParams(vmem_limit_bytes=48 * 2**20, **extra),
+            cost_estimate=pl.CostEstimate(flops=10**9, bytes_accessed=30_000_000, transcendentals=0),
         )(*args)
 
+    def semaphores(count):
+        return [pltpu.SemaphoreType.DMA((count,)), pltpu.SemaphoreType.DMA((count,))]
+
     places = contact_places(contact_colloid, units)
-    smem = pl.BlockSpec(memory_space=pltpu.SMEM)
-    turned = pl.pallas_call(
-        axis_kernel,
-        out_shape=jax.ShapeDtypeStruct(axis_index.shape, jnp.int32),
-        in_specs=[smem, vmem],
-        out_specs=vmem,
-        scratch_shapes=shift_scratch(axis_index.shape, jnp.int32)
-        + [pltpu.SemaphoreType.DMA((6,)), pltpu.SemaphoreType.DMA((6,))],
-        compiler_params=pltpu.CompilerParams(collective_id=0, has_side_effects=True),
-    )(grid_shift, axis_index)
-    axis0, axis1 = turned[0], turned[1]
-    mean0 = call(first_kernel, mean_shape, [acc], 10**9, particle_cells, velocities)
+    numbers = jax.ShapeDtypeStruct((nhi, nlo), jnp.int32)
+    mean0, axis0, axis1 = call(
+        first_kernel, (mean_shape, numbers, numbers),
+        [acc] + shift_scratch(axis_index.shape, jnp.int32) + semaphores(6), 0,
+        grid_shift, axis_index, particle_cells, velocities,
+    )
     v1, mean1 = call(
-        middle_kernel, (jax.ShapeDtypeStruct(velocities.shape, F32), mean_shape), [acc, table], 10**9,
-        particle_cells, velocities, mean0, axis0.reshape(nhi, nlo),
-    )
-    box = jax.ShapeDtypeStruct((8, max(units, 256)), F32)
-    outs = call(
+        middle_kernel, (jax.ShapeDtypeStruct(velocities.shape, F32), mean_shape), [acc, table], None,
+        particle_cells, velocities, mean0, axis0,
+    )
+    grid_mean = mean1.reshape(3, cx, cy, nlo)
+    return call(
         lambda t, h, l, *refs: last_kernel(t, h, l, units, *refs),
-        (jax.ShapeDtypeStruct((3, particles + 6 * CAP), F32),)
-        + (box,) * 6
-        + (jax.ShapeDtypeStruct((4, units), F32),),
-        [pltpu.VMEM((96, CAP), F32), table, pltpu.VMEM((3, particles // 128, 128), F32)],
-        10**9,
-        particle_cells, v1, mean1, axis1.reshape(nhi, nlo), migrate_dir.reshape(1, -1),
-        migrate_slot.reshape(1, -1), places.reshape(1, -1), contact_particle.reshape(1, -1),
-        contact_weight.reshape(1, -1),
-    )
-    mean_box = mean1.reshape(3, cx, cy, nlo)
-    cell_velocity, tail, force = pl.pallas_call(
-        functools.partial(tail_kernel, units),
-        out_shape=(
-            jax.ShapeDtypeStruct(mean_box.shape, F32),
-            jax.ShapeDtypeStruct((3, 6 * CAP), F32),
+        (
+            jax.ShapeDtypeStruct(grid_mean.shape, F32),
+            jax.ShapeDtypeStruct((3, particles + 6 * CAP), F32),
             jax.ShapeDtypeStruct((3, units), F32),
         ),
-        in_specs=[smem] + [vmem] * 9,
-        out_specs=(vmem, vmem, vmem),
-        scratch_shapes=shift_scratch(mean_box.shape, F32)
-        + [pltpu.VMEM((6,) + box.shape, F32)]
-        + [pltpu.SemaphoreType.DMA((12,)), pltpu.SemaphoreType.DMA((12,))],
-        compiler_params=pltpu.CompilerParams(collective_id=1, has_side_effects=True),
-    )(grid_shift, mean_box, *outs[1:8], colloid_velocity)
-    migrated = lax.dynamic_update_slice(outs[0], tail, (0, particles))
-    return (cell_velocity, migrated, force)
+        [pltpu.VMEM((96, CAP), F32), table, pltpu.VMEM((3, particles // 128, 128), F32)]
+        + [pltpu.VMEM((6, 3, CAP), F32)] * 2
+        + [pltpu.VMEM((6, 4, units), F32)] * 2
+        + shift_scratch(grid_mean.shape, F32)
+        + semaphores(18),
+        1,
+        grid_shift, grid_mean, particle_cells, v1, mean1, axis1, migrate_dir.reshape(1, -1),
+        migrate_slot.reshape(1, -1), places.reshape(1, -1), contact_particle.reshape(1, -1),
+        contact_weight.reshape(1, -1), colloid_velocity,
+    )
 
 
 def solution(mesh):

time: 86.4 us -> 61.4 us (0.71); the launches traced: 84.8 us -> 61.1 us
  Pallas kernels: 72.9 us -> 54.1 us
  local copies, waits for them, and re-layouts: 11 us -> 6.14 us
    pallas_call x2 -> x0, Pallas kernels: 28.4 us -> none  [the longest x1 15.2 us: body(): pl.pallas_call(axis_kernel, out_shape=jax.ShapeDtypeStruct(axis_index.sha...]
    pallas_call x3, Pallas kernels: 44.5 us -> 54.1 us  [call(): pl.pallas_call(functools.partial(kernel, tile, nhi, nlo), out_shape=outs,...]
    unnamed x34 -> x27, local copies, waits for them, and re-layouts: 8.94 us -> 6.14 us
    dynamic_update_slice x1 -> x0, local copies, waits for them, and re-layouts: 1.33 us -> none  [body(): migrated = lax.dynamic_update_slice(outs[0], tail, (0, particles))]
where the time goes in v3:
time: 61.4 us; the launch traced here: 61.1 us
  Pallas kernels  54.1 us (88%)
  local copies, waits for them, and re-layouts  6.14 us (10%)
  between operations  0.78 us (1%)
    pallas_call x3, Pallas kernels, call(): pl.pallas_call(functools.partial(kernel, tile, nhi, nlo), out_shape=outs,...  54.1 us
    unnamed x27, local copies, waits for them, and re-layouts  6.14 us

profile of v3, /device:TPU:0, one launch (start us, length us, event | category | flops | bytes accessed | tf_op | source)
XLA Modules:
  0.0 61.1 jit_solution(18210769824874343668)
XLA Ops:
  0.6 0.0 copy-start.11
  0.6 0.0 copy-start.6
  0.7 0.7 %copy-done.11 = s32[2048]{0:T(1024)S(1)} copy-done((s32[2048]{0:T(1024)S(1)}, s32[2048]{0:T(1024)}, u32[]{:S(2)}) %copy-start.11) | copy-done | bytes 8216
  1.4 0.0 copy-start.10
  1.4 0.0 copy-done.6
  1.4 0.7 %copy-done.10 = s32[2,3]{1,0:T(2,128)S(1)} copy-done((s32[2,3]{1,0:T(2,128)S(1)}, s32[2,3]{1,0:T(2,128)}, u32[]{:S(2)}) %copy-start.10) | copy-done | bytes 48
  2.1 0.0 copy-start
  2.1 1.1 %copy-done = f32[3,40960]{1,0:T(4,128)S(1)} copy-done((f32[3,40960]{1,0:T(4,128)S(1)}, f32[3,40960]{1,0:T(4,128)}, u32[]{:S(2)}) %copy-start) | copy-done | bytes 491544
  3.1 0.0 copy-start.2
  3.2 1.0 %copy-done.2 = s32[2,40960]{1,0:T(2,128)S(1)} copy-done((s32[2,40960]{1,0:T(2,128)S(1)}, s32[2,40960]{1,0:T(2,128)}, u32[]{:S(2)}) %copy-start.2) | copy-done | bytes 327704
  4.1 0.0 copy-start.1
  4.1 15.7 %shard_map.121 = (f32[3,32,128]{2,1,0:T(8,128)S(1)}, s32[32,128]{1,0:T(8,128)S(1)}, s32[32,128]{1,0:T(8,128)S(1)}) custom-call(s32[2,3]{1,0:T(2,128)S(1)} %copy-done.10, s32[2,4,8,128]{3,2,1,0:T(8,128)S(1)} %copy-done.6, s32[2,40960]{1,0:T(2,128)S(1)} %copy-done.2, f32[3,40960]{1,0:T(4,128)S(1)} %copy-done), custom_call_target="tpu_custom_call" | custom-call | flops 1000000000 | bytes 30000000 | tf_op jit(solution)/shard_map/pallas_call | solution.py:355
  19.8 0.0 copy-done.1
  19.8 0.0 copy-start.3
  19.8 0.0 copy-start.4
  19.8 0.0 copy-start.5
  19.8 0.0 copy-start.7
  19.8 0.0 copy-start.8
  19.9 16.5 %shard_map.122 = (f32[3,40960]{1,0:T(4,128)S(1)}, f32[3,32,128]{2,1,0:T(8,128)S(1)}) custom-call(s32[2,40960]{1,0:T(2,128)S(1)} %copy-done.2, f32[3,40960]{1,0:T(4,128)S(1)} %copy-done.1, f32[3,32,128]{2,1,0:T(8,128)S(1)} %get-tuple-element.8.mean_ref, s32[32,128]{1,0:T(8,128)S(1)} %get-tuple-element.9.axis_ref), custom_call_target="tpu_custom_call" | custom-call | flops 1000000000 | bytes 30000000 | tf_op jit(solution)/shard_map/pallas_call | solution.py:355
  36.4 0.0 copy-start.9
  36.4 0.0 copy-done.3
  36.4 0.0 copy-done.4
  36.4 0.0 copy-done.5
  36.4 0.0 copy-done.7
  36.4 0.0 copy-done.8
  36.4 0.6 %copy-done.9 = f32[3,256]{1,0:T(4,128)S(1)} copy-done((f32[3,256]{1,0:T(4,128)S(1)}, f32[3,256]{1,0:T(4,128)}, u32[]{:S(2)}) %copy-start.9) | copy-done | bytes 3096
  37.1 22.0 %shard_map.123 = (f32[3,4,8,128]{3,2,1,0:T(8,128)S(1)}, f32[3,41920]{1,0:T(4,128)S(1)}, f32[3,256]{1,0:T(4,128)S(1)}) custom-call(s32[2,3]{1,0:T(2,128)S(1)} %copy-done.10, f32[3,4,8,128]{3,2,1,0:T(8,128)S(1)} %bitcast.11, s32[2,40960]{1,0:T(2,128)S(1)} %copy-done.3, f32[3,40960]{1,0:T(4,128)S(1)} %get-tuple-element.11.refs_3_, ...), custom_call_target="tpu_custom_call" | custom-call | flops 1000000000 | bytes 30000000 | tf_op jit(solution)/shard_map/pallas_call | solution.py:355
  59.0 0.6 %copy.16 = f32[3,4,8,128]{3,2,1,0:T(8,128)} copy(f32[3,4,8,128]{3,2,1,0:T(8,128)S(1)} %get-tuple-element.16) | data formatting | bytes 98304
  59.7 0.8 %copy.17 = f32[3,41920]{1,0:T(4,128)} copy(f32[3,41920]{1,0:T(4,128)S(1)} %get-tuple-element.17) | data formatting | bytes 1006080
  60.5 0.6 copy.18
  (1 shorter events, 0.0 us)
Async XLA Ops:
  0.6 0.7 %copy-start.11 = (s32[2048]{0:T(1024)S(1)}, s32[2048]{0:T(1024)}, u32[]{:S(2)}) copy-start(s32[2048]{0:T(1024)} %param.16) | copy-start | bytes 24580
  0.6 0.8 %copy-start.6 = (s32[2,4,8,128]{3,2,1,0:T(8,128)S(1)}, s32[2,4,8,128]{3,2,1,0:T(8,128)}, u32[]{:S(2)}) copy-start(s32[2,4,8,128]{3,2,1,0:T(8,128)} %x_ref.1) | copy-start | bytes 98308
  1.4 0.7 %copy-start.10 = (s32[2,3]{1,0:T(2,128)S(1)}, s32[2,3]{1,0:T(2,128)}, u32[]{:S(2)}) copy-start(s32[2,3]{1,0:T(2,128)} %refs_0_.1) | copy-start | bytes 76
  2.1 1.1 %copy-start = (f32[3,40960]{1,0:T(4,128)S(1)}, f32[3,40960]{1,0:T(4,128)}, u32[]{:S(2)}) copy-start(f32[3,40960]{1,0:T(4,128)} %v_ref.3) | copy-start | bytes 1474564
  3.1 1.0 %copy-start.2 = (s32[2,40960]{1,0:T(2,128)S(1)}, s32[2,40960]{1,0:T(2,128)}, u32[]{:S(2)}) copy-start(s32[2,40960]{1,0:T(2,128)} %refs_2_.1) | copy-start | bytes 983044
  4.1 15.7 %copy-start.1 = (f32[3,40960]{1,0:T(4,128)S(1)}, f32[3,40960]{1,0:T(4,128)}, u32[]{:S(2)}) copy-start(f32[3,40960]{1,0:T(4,128)} %v_ref.3) | copy-start | bytes 1474564
  19.8 16.6 %copy-start.3 = (s32[2,40960]{1,0:T(2,128)S(1)}, s32[2,40960]{1,0:T(2,128)}, u32[]{:S(2)}) copy-start(s32[2,40960]{1,0:T(2,128)} %refs_2_.1) | copy-start | bytes 983044
  19.8 16.6 %copy-start.4 = (s32[40960]{0:T(1024)S(1)}, s32[40960]{0:T(1024)}, u32[]{:S(2)}) copy-start(s32[40960]{0:T(1024)} %param.14) | copy-start | bytes 491524
  19.8 16.6 %copy-start.5 = (s32[40960]{0:T(1024)S(1)}, s32[40960]{0:T(1024)}, u32[]{:S(2)}) copy-start(s32[40960]{0:T(1024)} %param.15) | copy-start | bytes 491524
  19.8 16.6 %copy-start.7 = (s32[2048]{0:T(1024)S(1)}, s32[2048]{0:T(1024)}, u32[]{:S(2)}) copy-start(s32[2048]{0:T(1024)} %param.17) | copy-start | bytes 24580
  19.8 16.6 %copy-start.8 = (f32[2048]{0:T(1024)S(1)}, f32[2048]{0:T(1024)}, u32[]{:S(2)}) copy-start(f32[2048]{0:T(1024)} %param.18) | copy-start | bytes 24580
  36.4 0.7 %copy-start.9 = (f32[3,256]{1,0:T(4,128)S(1)}, f32[3,256]{1,0:T(4,128)}, u32[]{:S(2)}) copy-start(f32[3,256]{1,0:T(4,128)} %refs_11_.1) | copy-start | bytes 9220

commit v4 on v3

--- a/solution.py
+++ b/solution.py
@@ -11,7 +11,7 @@
 CAP = 160
 ANGLE = 130.0 * math.pi / 180.0
 COS, SIN = math.cos(ANGLE), math.sin(ANGLE)
-TILE = 2048
+TILE = 4096
 NT = (((1,), (1,)), ((), ()))
 BF = jnp.bfloat16
 F32 = jnp.float32

time: 61.4 us -> 56.5 us (0.920)
  Pallas kernels: 54.1 us -> 49.2 us
    pallas_call x3, Pallas kernels: 54.1 us -> 49.2 us  [call(): pl.pallas_call(functools.partial(kernel, tile, nhi, nlo), out_shape=outs,...]
where the time goes in v4:
time: 56.5 us; the launch traced here: 56.2 us
  Pallas kernels  49.2 us (87%)
  local copies, waits for them, and re-layouts  6.14 us (11%)
  between operations  0.78 us (1%)
    pallas_call x3, Pallas kernels, call(): pl.pallas_call(functools.partial(kernel, tile, nhi, nlo), out_shape=outs,...  49.2 us
    unnamed x27, local copies, waits for them, and re-layouts  6.14 us

profile of v4, /device:TPU:0, one launch (start us, length us, event | category | flops | bytes accessed | tf_op | source)
XLA Modules:
  0.0 56.2 jit_solution(14977369665164153117)
XLA Ops:
  0.6 0.0 copy-start.11
  0.6 0.0 copy-start.6
  0.7 0.7 %copy-done.11 = s32[2048]{0:T(1024)S(1)} copy-done((s32[2048]{0:T(1024)S(1)}, s32[2048]{0:T(1024)}, u32[]{:S(2)}) %copy-start.11) | copy-done | bytes 8216
  1.4 0.0 copy-start.10
  1.4 0.0 copy-done.6
  1.4 0.7 %copy-done.10 = s32[2,3]{1,0:T(2,128)S(1)} copy-done((s32[2,3]{1,0:T(2,128)S(1)}, s32[2,3]{1,0:T(2,128)}, u32[]{:S(2)}) %copy-start.10) | copy-done | bytes 48
  2.1 0.0 copy-start
  2.1 1.1 %copy-done = f32[3,40960]{1,0:T(4,128)S(1)} copy-done((f32[3,40960]{1,0:T(4,128)S(1)}, f32[3,40960]{1,0:T(4,128)}, u32[]{:S(2)}) %copy-start) | copy-done | bytes 491544
  3.1 0.0 copy-start.2
  3.2 1.0 %copy-done.2 = s32[2,40960]{1,0:T(2,128)S(1)} copy-done((s32[2,40960]{1,0:T(2,128)S(1)}, s32[2,40960]{1,0:T(2,128)}, u32[]{:S(2)}) %copy-start.2) | copy-done | bytes 327704
  4.1 0.0 copy-start.1
  4.1 15.0 %shard_map.121 = (f32[3,32,128]{2,1,0:T(8,128)S(1)}, s32[32,128]{1,0:T(8,128)S(1)}, s32[32,128]{1,0:T(8,128)S(1)}) custom-call(s32[2,3]{1,0:T(2,128)S(1)} %copy-done.10, s32[2,4,8,128]{3,2,1,0:T(8,128)S(1)} %copy-done.6, s32[2,40960]{1,0:T(2,128)S(1)} %copy-done.2, f32[3,40960]{1,0:T(4,128)S(1)} %copy-done), custom_call_target="tpu_custom_call" | custom-call | flops 1000000000 | bytes 30000000 | tf_op jit(solution)/shard_map/pallas_call | solution.py:355
  19.1 0.0 copy-done.1
  19.2 0.0 copy-start.3
  19.2 0.0 copy-start.4
  19.2 0.0 copy-start.5
  19.2 0.0 copy-start.7
  19.2 0.0 copy-start.8
  19.2 13.8 %shard_map.122 = (f32[3,40960]{1,0:T(4,128)S(1)}, f32[3,32,128]{2,1,0:T(8,128)S(1)}) custom-call(s32[2,40960]{1,0:T(2,128)S(1)} %copy-done.2, f32[3,40960]{1,0:T(4,128)S(1)} %copy-done.1, f32[3,32,128]{2,1,0:T(8,128)S(1)} %get-tuple-element.8.mean_ref, s32[32,128]{1,0:T(8,128)S(1)} %get-tuple-element.9.axis_ref), custom_call_target="tpu_custom_call" | custom-call | flops 1000000000 | bytes 30000000 | tf_op jit(solution)/shard_map/pallas_call | solution.py:355
  33.0 0.0 copy-start.9
  33.0 0.0 copy-done.3
  33.0 0.0 copy-done.4
  33.0 0.0 copy-done.5
  33.0 0.0 copy-done.7
  33.1 0.0 copy-done.8
  33.1 0.6 %copy-done.9 = f32[3,256]{1,0:T(4,128)S(1)} copy-done((f32[3,256]{1,0:T(4,128)S(1)}, f32[3,256]{1,0:T(4,128)}, u32[]{:S(2)}) %copy-start.9) | copy-done | bytes 3096
  33.7 20.4 %shard_map.123 = (f32[3,4,8,128]{3,2,1,0:T(8,128)S(1)}, f32[3,41920]{1,0:T(4,128)S(1)}, f32[3,256]{1,0:T(4,128)S(1)}) custom-call(s32[2,3]{1,0:T(2,128)S(1)} %copy-done.10, f32[3,4,8,128]{3,2,1,0:T(8,128)S(1)} %bitcast.11, s32[2,40960]{1,0:T(2,128)S(1)} %copy-done.3, f32[3,40960]{1,0:T(4,128)S(1)} %get-tuple-element.11.refs_3_, ...), custom_call_target="tpu_custom_call" | custom-call | flops 1000000000 | bytes 30000000 | tf_op jit(solution)/shard_map/pallas_call | solution.py:355
  54.1 0.6 %copy.16 = f32[3,4,8,128]{3,2,1,0:T(8,128)} copy(f32[3,4,8,128]{3,2,1,0:T(8,128)S(1)} %get-tuple-element.16) | data formatting | bytes 98304
  54.7 0.8 %copy.17 = f32[3,41920]{1,0:T(4,128)} copy(f32[3,41920]{1,0:T(4,128)S(1)} %get-tuple-element.17) | data formatting | bytes 1006080
  55.6 0.6 %copy.18 = f32[3,256]{1,0:T(4,128)} copy(f32[3,256]{1,0:T(4,128)S(1)} %get-tuple-element.18) | data formatting | bytes 6144
  (1 shorter events, 0.0 us)
Async XLA Ops:
  0.6 0.7 %copy-start.11 = (s32[2048]{0:T(1024)S(1)}, s32[2048]{0:T(1024)}, u32[]{:S(2)}) copy-start(s32[2048]{0:T(1024)} %param.16) | copy-start | bytes 24580
  0.6 0.8 %copy-start.6 = (s32[2,4,8,128]{3,2,1,0:T(8,128)S(1)}, s32[2,4,8,128]{3,2,1,0:T(8,128)}, u32[]{:S(2)}) copy-start(s32[2,4,8,128]{3,2,1,0:T(8,128)} %x_ref.1) | copy-start | bytes 98308
  1.4 0.7 %copy-start.10 = (s32[2,3]{1,0:T(2,128)S(1)}, s32[2,3]{1,0:T(2,128)}, u32[]{:S(2)}) copy-start(s32[2,3]{1,0:T(2,128)} %refs_0_.1) | copy-start | bytes 76
  2.1 1.1 %copy-start = (f32[3,40960]{1,0:T(4,128)S(1)}, f32[3,40960]{1,0:T(4,128)}, u32[]{:S(2)}) copy-start(f32[3,40960]{1,0:T(4,128)} %v_ref.3) | copy-start | bytes 1474564
  3.1 1.0 %copy-start.2 = (s32[2,40960]{1,0:T(2,128)S(1)}, s32[2,40960]{1,0:T(2,128)}, u32[]{:S(2)}) copy-start(s32[2,40960]{1,0:T(2,128)} %refs_2_.1) | copy-start | bytes 983044
  4.1 15.0 %copy-start.1 = (f32[3,40960]{1,0:T(4,128)S(1)}, f32[3,40960]{1,0:T(4,128)}, u32[]{:S(2)}) copy-start(f32[3,40960]{1,0:T(4,128)} %v_ref.3) | copy-start | bytes 1474564
  19.2 13.9 %copy-start.3 = (s32[2,40960]{1,0:T(2,128)S(1)}, s32[2,40960]{1,0:T(2,128)}, u32[]{:S(2)}) copy-start(s32[2,40960]{1,0:T(2,128)} %refs_2_.1) | copy-start | bytes 983044
  19.2 13.9 %copy-start.4 = (s32[40960]{0:T(1024)S(1)}, s32[40960]{0:T(1024)}, u32[]{:S(2)}) copy-start(s32[40960]{0:T(1024)} %param.14) | copy-start | bytes 491524
  19.2 13.9 %copy-start.5 = (s32[40960]{0:T(1024)S(1)}, s32[40960]{0:T(1024)}, u32[]{:S(2)}) copy-start(s32[40960]{0:T(1024)} %param.15) | copy-start | bytes 491524
  19.2 13.9 %copy-start.7 = (s32[2048]{0:T(1024)S(1)}, s32[2048]{0:T(1024)}, u32[]{:S(2)}) copy-start(s32[2048]{0:T(1024)} %param.17) | copy-start | bytes 24580
  19.2 13.9 %copy-start.8 = (f32[2048]{0:T(1024)S(1)}, f32[2048]{0:T(1024)}, u32[]{:S(2)}) copy-start(f32[2048]{0:T(1024)} %param.18) | copy-start | bytes 24580
  33.0 0.7 %copy-start.9 = (f32[3,256]{1,0:T(4,128)S(1)}, f32[3,256]{1,0:T(4,128)}, u32[]{:S(2)}) copy-start(f32[3,256]{1,0:T(4,128)} %refs_11_.1) | copy-start | bytes 9220
